TPU v7x, 32 devices: a whole 2x2x4 slice. The times are simulated.
32 devices in a mesh: bus: 8 (over y, x, core), period: 4 (over z).
Axes of the slice: x: 2, y: 2, z: 4, core: 2. Of those that a mesh axis runs over, the one named last changes fastest.
Arguments:
- deviation: bfloat16 [128, 256, 128], P('bus', 'period'), may hold values from -6 to 6
- loading: bfloat16 [128, 256, 128], P('bus', 'period'), may hold values from 0.5 to 2
- jacobian: bfloat16 [128, 128, 128], P('bus'), may hold values from -0.5 to 0.5
- tie_source: int32 [128, 16], P('bus'), may hold values from 0 to 127
- tie_target: int32 [128, 16], P('bus'), may hold values from 0 to 127
- tie_admittance: float32 [128, 16], P('bus'), may hold values from 0.5 to 2
- condense: bfloat16 [128, 128, 512], P('bus'), may hold values from -0.046875 to 0.046875
- section_gain: bfloat16 [4, 64, 512, 512], P('period', 'bus'), may hold values from -0.0625 to 0.0625
- retention: float32 [4, 64, 512], P('period', 'bus'), may hold values from 0 to 1
Outputs:
- mismatch: bfloat16 [128, 256, 128], P('bus', 'period')
- section_states: float32 [4, 64, 512], P('period', 'bus')
All inputs are finite; a program needn't handle non-finite values.
Results may differ from a plain program's by a relative error of at most 0.013.
Values may be sent and summed in bfloat16 or wider, within the bound.
No kernel may reach another device: no remote copies, remote signals or barrier semaphores. Data moves between devices by JAX's collectives and lax.ppermute only.
A program may use at most 64 MiB of HBM per device.

v0:
```python
import jax
import jax.numpy as jnp
from jax import lax
from jax.sharding import PartitionSpec as P


def from_behind(value, axis, steps):
    count = lax.axis_size(axis)
    leading, last = (max(0, -steps), min(count, count - steps))
    return lax.ppermute(value, axis, [(source, source + steps) for source in range(leading, last)])


def entering_2(value, axis, combine, identity):
    size, place = (lax.axis_size(axis), lax.axis_index(axis))
    everything = jax.tree.map(lambda part: lax.all_gather(part, axis), value)
    start = jax.tree.map(
        lambda part, zero: jnp.broadcast_to(jnp.asarray(zero, part.dtype), part.shape),
        value,
        identity,
    )

    def step(k, before):
        reached = k < place
        new = combine(before, jax.tree.map(lambda part: part[k], everything))
        return jax.tree.map(lambda a, b: jnp.where(reached, a, b), new, before)

    return lax.fori_loop(0, size, step, start)


def broadcast(block, axis, owner):
    block = jnp.where(lax.axis_index(axis) == owner, block, jnp.zeros_like(block))
    return lax.psum(block, axis)


def combine(earlier, later):
    return (earlier[0] * later[0], later[0] * earlier[1] + later[1])


def place(flows, hot):
    upper = flows.astype(jnp.bfloat16)
    lower = (flows - upper.astype(jnp.float32)).astype(jnp.bfloat16)
    both = jnp.concatenate([upper, lower], axis=2)
    hot_twice = jnp.concatenate([hot, hot], axis=1)
    return jnp.einsum("bte,beq->btq", both, hot_twice, preferred_element_type=jnp.float32)


def shards(
    deviation,
    loading,
    jacobian,
    tie_source,
    tie_target,
    tie_admittance,
    condense,
    section_gain,
    retention,
):
    block_width = deviation.shape[2]
    scaled = (deviation.astype(jnp.float32) * loading.astype(jnp.float32)).astype(jnp.bfloat16)
    columns = jnp.arange(block_width, dtype=jnp.int32)
    source_hot = (tie_source[:, :, None] == columns[None, None, :]).astype(jnp.bfloat16)
    target_hot = (tie_target[:, :, None] == columns[None, None, :]).astype(jnp.bfloat16)
    next_first = from_behind(scaled[0], "bus", -1)
    next_block = jnp.concatenate([scaled[1:], next_first[None]], axis=0)
    at_target = jnp.einsum(
        "btq,beq->bte", next_block, target_hot, preferred_element_type=jnp.float32
    )
    network = jnp.einsum("btp,bpq->btq", scaled, jacobian, preferred_element_type=jnp.float32)
    at_source = jnp.einsum("btq,beq->bte", scaled, source_hot, preferred_element_type=jnp.float32)
    edge_flow = tie_admittance[:, None, :] * (at_target - at_source)
    own_terms = place(edge_flow, source_hot)
    handed = -place(edge_flow, target_hot)
    incoming = from_behind(handed[-1], "bus", 1)
    received = jnp.concatenate([incoming[None], handed[:-1]], axis=0)
    mismatch = (network + own_terms + received).astype(jnp.bfloat16)
    span_rows = section_gain.shape[1]
    partial_value = jnp.einsum(
        "btq,bqm->tm", mismatch, condense, preferred_element_type=jnp.float32
    )
    totals = lax.psum(partial_value, "bus")
    section_sum = lax.dynamic_slice_in_dim(totals, lax.axis_index("bus") * span_rows, span_rows, 0)
    section_in = section_sum.astype(jnp.bfloat16)
    pushed = jnp.einsum(
        "tm,tmn->tn", section_in, section_gain[0], preferred_element_type=jnp.float32
    )
    states_width = pushed.shape[1]
    ones_row = jnp.ones((states_width,), jnp.float32)
    zeros_row = jnp.zeros((states_width,), jnp.float32)

    def advance(carried, inputs):
        section_now, product = carried
        retain, pushed_now = inputs
        section_now = retain * section_now + pushed_now
        product = product * retain
        return ((section_now, product), (section_now, product))

    (last_state, span_rate), (local_states, running) = lax.scan(
        advance, (zeros_row, ones_row), (retention[0], pushed)
    )
    own_map = (span_rate, last_state)
    identity = (ones_row, zeros_row)
    before = entering_2(own_map, "bus", combine, identity)
    through = combine(before, own_map)
    group_map = (
        broadcast(through[0], "bus", lax.axis_size("bus") - 1),
        broadcast(through[1], "bus", lax.axis_size("bus") - 1),
    )
    across = entering_2(group_map, "period", combine, identity)
    entering = combine(across, before)[1]
    states = local_states + running * entering[None, :]
    return (mismatch, states[None])


def solution(mesh):
    placed = (
        P("bus", "period", None),
        P("bus", "period", None),
        P("bus", None, None),
        P("bus", None),
        P("bus", None),
        P("bus", None),
        P("bus", None, None),
        P("period", "bus", None, None),
        P("period", "bus", None),
    )
    return jax.shard_map(
        shards,
        mesh=mesh,
        in_specs=placed,
        out_specs=(P("bus", "period", None), P("period", "bus", None)),
        check_vma=False,
    )
```

profile of v0, /device:TPU:0, one launch (start us, length us, event | category | flops | bytes accessed | tf_op | source)
XLA Modules:
  0.0 106.2 jit_solution(14670595446566683150)
XLA Ops:
  0.6 0.0 copy-start
  0.7 1.3 %multiply_convert_fusion = bf16[16,64,128]{2,1,0:T(8,128)(2,1)S(1)} fusion(bf16[16,64,128]{2,1,0:T(8,128)(2,1)} %param.16, bf16[16,64,128]{2,1,0:T(8,128)(2,1)} %param.15), kind=kLoop, calls=%fused_computation.21 | loop fusion | flops 524288 | bytes 786432 | tf_op jit(solution)/shard_map/convert_element_type | solution.py:59
  1.9 1.3 %collective-permute-start = (bf16[64,128]{1,0:T(8,128)(2,1)S(1)}, bf16[64,128]{1,0:T(8,128)(2,1)S(1)}, u32[]{:S(2)}, u32[]{:S(2)}) collective-permute-start(bf16[64,128]{1,0:T(8,128)(2,1)S(1)} %slice_bitcast_fusion.1), channel_id=1, source_target_pairs={{4,0},{8,4},{12,8},{16,12},{20,16},{24,20},{28,24},{5,1},{9,5},{13... | collective-permute-start | bytes 49160 | tf_op jit(solution)/shard_map/ppermute | solution.py:10
  3.2 1.0 fusion.23
  4.2 1.3 %fusion.25 = f32[16,64,128]{2,1,0:T(8,128)S(1)} fusion(bf16[16,64,128]{2,1,0:T(8,128)(2,1)S(1)} %multiply_convert_fusion, bf16[16,128,128]{2,1,0:T(8,128)(2,1)} %param.17), kind=kOutput, calls=%fused_computation.56 | convolution fusion | flops 33554432 | bytes 1310720 | tf_op jit(solution)/shard_map/btp,bpq->btq/dot_general | solution.py:68
  5.5 0.8 iota_compare_fusion.1
  6.4 1.0 fusion.24
  7.4 0.3 convolution_negate_fusion
  7.7 3.8 %collective-permute-start.1 = (f32[64,128]{1,0:T(8,128)S(1)}, f32[64,128]{1,0:T(8,128)S(1)}, u32[]{:S(2)}, u32[]{:S(2)}) collective-permute-start(f32[64,128]{1,0:T(8,128)S(1)} %slice_bitcast_fusion), channel_id=1, source_target_pairs={{0,4},{4,8},{8,12},{12,16},{16,20},{20,24},{24,28},{1,5},{5,9},{9,... | collective-permute-start | bytes 98312 | tf_op jit(solution)/shard_map/ppermute | solution.py:10
  11.5 0.1 iota_compare_fusion
  11.8 0.6 collective-permute-done.1
  12.4 0.3 fusion.4
  12.7 0.5 convolution_bitcast_fusion
  13.2 26.5 %all-reduce.2 = bf16[64,512]{1,0:T(8,128)(2,1)S(1)} all-reduce(f32[64,512]{1,0:T(8,128)S(1)} %convolution_bitcast_fusion), channel_id=1, replica_groups=mesh['bus'=8,'period'=4] {'bus'}, use_global_device_ids=true, to_apply=%region_0.0 | all-reduce | flops 32768 | bytes 196608 | tf_op jit(solution)/shard_map/psum | solution.py:80
  39.7 2.8 %fusion.1 = f32[8,1,512]{2,1,0:T(1,128)S(1)} fusion(bf16[1,8,512,512]{3,2,1,0:T(8,128)(2,1)} %param.22, bf16[8,512,1]{1,0,2:T(8,128)(2,1)S(1)} %fusion.17), kind=kOutput, calls=%fused_computation.12 | convolution fusion | flops 4194304 | bytes 4218880 | tf_op jit(solution)/shard_map/tm,tmn->tn/dot_general | solution.py:83
  42.5 7.1 %while.47 = (s32[]{:T(128)}, f32[512]{0:T(512)S(1)}, f32[512]{0:T(512)S(1)}, f32[8,512]{1,0:T(8,128)S(1)}, f32[8,512]{1,0:T(8,128)S(1)}, /*index=5*/f32[8,512]{1...) while((s32[]{:T(128)}, f32[512]{0:T(512)S(1)}, f32[512]{0:T(512)S(1)}, f32[8,512]{1,0:T(8,128)S(1)}, ...), condition=%wide.region_2.3_spmd.clone, body=%wide.region_1.2_spmd.clone.sunk | while | flops 2563 | bytes 28787 | solution.py:97
  42.5 0.7 constant_dynamic-slice_fusion.9
  43.3 0.1 dynamic_update_slice.12
  43.3 0.1 dynamic_update_slice.11
  43.4 0.7 constant_dynamic-slice_fusion.9
  44.2 0.1 dynamic_update_slice.12
  44.2 0.1 dynamic_update_slice.11
  44.3 0.7 constant_dynamic-slice_fusion.9
  45.0 0.1 dynamic_update_slice.12
  45.1 0.1 dynamic_update_slice.11
  45.2 0.7 constant_dynamic-slice_fusion.9
  45.9 0.1 dynamic_update_slice.12
  46.0 0.1 dynamic_update_slice.11
  46.1 0.7 constant_dynamic-slice_fusion.9
  46.8 0.1 dynamic_update_slice.12
  46.9 0.1 dynamic_update_slice.11
  47.0 0.7 constant_dynamic-slice_fusion.9
  47.7 0.1 dynamic_update_slice.12
  47.8 0.1 dynamic_update_slice.11
  47.9 0.7 constant_dynamic-slice_fusion.9
  48.6 0.1 dynamic_update_slice.12
  48.7 0.1 dynamic_update_slice.11
  48.8 0.7 constant_dynamic-slice_fusion.9
  49.5 0.1 dynamic_update_slice.12
  49.6 0.1 dynamic_update_slice.11
  49.7 10.4 %all-gather.3 = f32[8,1,512]{2,1,0:T(1,128)S(1)} all-gather(f32[1,1,512]{2,1,0:T(1,128)S(1)} %bitcast.67), channel_id=3, replica_groups=mesh['bus'=8,'period'=4] {'bus'}, dimensions={0}, use_global_device_ids=true | all-gather | bytes 18432 | tf_op jit(solution)/shard_map/all_gather | solution.py:15
  60.0 7.7 %all-gather.2 = f32[8,1,512]{2,1,0:T(1,128)S(1)} all-gather(f32[1,1,512]{2,1,0:T(1,128)S(1)} %bitcast.69), channel_id=2, replica_groups=mesh['bus'=8,'period'=4] {'bus'}, dimensions={0}, use_global_device_ids=true | all-gather | bytes 18432 | tf_op jit(solution)/shard_map/all_gather | solution.py:15
  67.7 0.4 while.48
  68.2 13.2 %all-reduce = (f32[1,512]{1,0:T(1,128)S(1)}, f32[1,512]{1,0:T(1,128)S(1)}) all-reduce(f32[1,512]{1,0:T(1,128)S(1)} %bitcast.83, f32[1,512]{1,0:T(1,128)S(1)} %bitcast.82), channel_id=1, replica_groups=mesh['bus'=8,'period'=4] {'bus'}, use_global_device_ids=true, to_apply=%region_5.6 | all-reduce | flops 1024 | bytes 8192 | tf_op jit(solution)/shard_map/psum | solution.py:32
  81.4 12.1 %all-gather.5 = f32[4,1,512]{2,1,0:T(1,128)S(1)} all-gather(f32[1,1,512]{2,1,0:T(1,128)S(1)} %bitcast.86), channel_id=1, replica_groups=mesh['bus'=8,'period'=4] {'period'}, dimensions={0}, use_global_device_ids=true | all-gather | bytes 10240 | tf_op jit(solution)/shard_map/all_gather | solution.py:15
  93.5 11.9 %all-gather.4 = f32[4,1,512]{2,1,0:T(1,128)S(1)} all-gather(f32[1,1,512]{2,1,0:T(1,128)S(1)} %bitcast.85), channel_id=1, replica_groups=mesh['bus'=8,'period'=4] {'period'}, dimensions={0}, use_global_device_ids=true | all-gather | bytes 10240 | tf_op jit(solution)/shard_map/all_gather | solution.py:15
  105.3 0.2 while.49
  105.6 0.6 add_bitcast_fusion
  (57 shorter events, 0.5 us)
Async XLA Ops:
  0.6 12.0 %copy-start = (bf16[16,128,512]{2,1,0:T(8,128)(2,1)S(1)}, bf16[16,128,512]{2,1,0:T(8,128)(2,1)}, u32[]{:S(2)}) copy-start(bf16[16,128,512]{2,1,0:T(8,128)(2,1)} %param.21) | copy-start | bytes 6291460
  0.6 10.9 %copy-start.2 = (s32[16,16]{1,0:T(8,128)S(1)}, s32[16,16]{1,0:T(8,128)}, u32[]{:S(2)}) copy-start(s32[16,16]{1,0:T(8,128)} %param.18) | copy-start | bytes 3076
  1.9 4.5 %collective-permute-start = (bf16[64,128]{1,0:T(8,128)(2,1)S(1)}, bf16[64,128]{1,0:T(8,128)(2,1)S(1)}, u32[]{:S(2)}, u32[]{:S(2)}) collective-permute-start(bf16[64,128]{1,0:T(8,128)(2,1)S(1)} %slice_bitcast_fusion.1), channel_id=1, source_target_pairs={{4,0},{8,4},{12,8},{16,12},{20,16},{24,20},{28,24},{5,1},{9,5},{13... | collective-permute-start | bytes 49160 | tf_op jit(solution)/shard_map/ppermute | solution.py:10
  7.7 4.7 %collective-permute-start.1 = (f32[64,128]{1,0:T(8,128)S(1)}, f32[64,128]{1,0:T(8,128)S(1)}, u32[]{:S(2)}, u32[]{:S(2)}) collective-permute-start(f32[64,128]{1,0:T(8,128)S(1)} %slice_bitcast_fusion), channel_id=1, source_target_pairs={{0,4},{4,8},{8,12},{12,16},{16,20},{20,24},{24,28},{1,5},{5,9},{9,... | collective-permute-start | bytes 98312 | tf_op jit(solution)/shard_map/ppermute | solution.py:10
  12.7 93.5 %copy-start.1 = (bf16[16,64,128]{2,1,0:T(8,128)(2,1)}, bf16[16,64,128]{2,1,0:T(8,128)(2,1)S(1)}, u32[]{:S(2)}) copy-start(bf16[16,64,128]{2,1,0:T(8,128)(2,1)S(1)} %fusion.4) | copy-start | bytes 786436
where the time goes:
time: 107 us; the launch traced here: 106 us
  blocking collectives  81.7 us (76%)
  matrix products  7.18 us (7%)
  local copies, waits for them, and re-layouts  7.02 us (7%)
  starting transfers between devices  5.11 us (5%)
  other arithmetic  3.07 us (3%)
    all_gather x4, blocking collectives, entering_2(): everything = jax.tree.map(lambda part: lax.all_gather(part, axis), value)  42 us
    psum x1, blocking collectives, shards(): totals = lax.psum(partial_value, 'bus')  26.5 us
    psum x1, blocking collectives, broadcast(): return lax.psum(block, axis)  13.2 us
    dynamic_slice x8, local copies, waits for them, and re-layouts, shards(): lax.scan(advance, (zeros_row, ones_row), (retention[0], pushed))  5.84 us
    ppermute x2, starting transfers between devices, from_behind(): lax.ppermute(value, axis, [(source, source + steps) for source in range(l...  5.11 us
    dot_general x1, matrix products, shards(): jnp.einsum('tm,tmn->tn', section_in, section_gain[0], preferred_element_t...  2.83 us
  transfers between devices with their start and end apart: 2, of which 1 were waited for; matrix products, arithmetic and copies ran while one was open for 3% of the time, Pallas kernels for 0%

commit v1 on v0

v1 whole, which is shorter than its diff:
```python
import jax
import jax.numpy as jnp
from jax import lax
from jax.experimental import pallas as pl
from jax.experimental.pallas import tpu as pltpu
from jax.sharding import PartitionSpec as P

F32, BF16, I32 = jnp.float32, jnp.bfloat16, jnp.int32
VM = pl.BlockSpec(memory_space=pltpu.VMEM)
TIE_ROWS = 16
PARAMS = pltpu.CompilerParams(vmem_limit_bytes=48 * 1024 * 1024)


def dot(a, b):
    return jnp.dot(a, b, preferred_element_type=F32)


def dot_t(a, b):
    return lax.dot_general(a, b, (((1,), (1,)), ((), ())), preferred_element_type=F32)


def product(deviation, loading):
    return (deviation.astype(F32) * loading.astype(F32)).astype(BF16)


def hot_columns(index_row, width):
    rows = lax.broadcasted_iota(I32, (width, index_row.shape[1]), 0)
    return (rows == index_row).astype(F32).astype(BF16)


def halves(flow, edges):
    upper = flow.astype(BF16).astype(F32)
    lane = lax.broadcasted_iota(I32, flow.shape, 1)
    return jnp.where(lane % (2 * edges) < edges, upper, flow - upper).astype(BF16)


def row_chunks(total, size, body):
    if total <= size:
        body(pl.ds(0, total))
        return

    @pl.loop(0, total // size)
    def _(k):
        body(pl.ds(pl.multiple_of(k * size, size), size))


def halo_kernel(dev, load, src, tgt, adm, pair_out, chip_out, ties):
    blocks, rows, _ = dev.shape
    edges = src.shape[1]
    last = blocks - 1
    even = lax.axis_index("bus") % 2 == 0
    ties[...] = jnp.zeros_like(ties)
    a = adm[last : last + 1, :]
    high = a.astype(BF16).astype(F32)
    mid = (a - high).astype(BF16).astype(F32)
    ties[0:1, 0:edges] = src[last : last + 1, :].astype(F32)
    ties[1:2, 0:edges] = tgt[last : last + 1, :].astype(F32)
    ties[2:3, 0:edges] = high
    ties[3:4, 0:edges] = mid
    ties[4:5, 0:edges] = a - high - mid
    packed = ties[...].astype(BF16)

    @pl.when(even)
    def _():
        pair_out[0:rows, :] = product(dev[last], load[last])
        chip_out[0:rows, :] = product(dev[0], load[0])

    @pl.when(jnp.logical_not(even))
    def _():
        pair_out[0:rows, :] = product(dev[0], load[0])
        chip_out[0:rows, :] = product(dev[last], load[last])

    pair_out[rows : rows + TIE_ROWS, :] = packed
    chip_out[rows : rows + TIE_ROWS, :] = packed


def inner_kernel(dev, load, jac, src, tgt, adm, cond, mis, ends, part):
    blocks, total, width = dev.shape
    edges = src.shape[1]
    src4 = jnp.concatenate([src[...]] * 4, axis=1)
    tgt4 = jnp.concatenate([tgt[...]] * 4, axis=1)
    adm4 = jnp.concatenate([adm[...]] * 4, axis=1)
    low = lax.broadcasted_iota(I32, (1, 4 * edges), 1) < 2 * edges
    hots = []
    for b in range(blocks):
        before = tgt4[b - 1 : b] if b else jnp.full((1, 4 * edges), -1, I32)
        mine = src4[b : b + 1]
        hots.append(hot_columns(jnp.where(low, *((before, mine) if b % 2 else (mine, before))), width))

    def body(here):
        scaled = [product(dev[b, here, :], load[b, here, :]) for b in range(blocks)]
        picked = [dot(scaled[b], hots[b]) for b in range(blocks)]
        previous = None
        row = []
        for b in range(blocks):
            after = picked[b + 1] if b + 1 < blocks else 0.0
            flow = adm4[b : b + 1] * (after - picked[b])
            received = 0.0 if previous is None else -previous
            flows = halves(jnp.where(low, *((received, flow) if b % 2 else (flow, received))), edges)
            previous = flow
            whole = dot(scaled[b], jac[b]) + dot_t(flows, hots[b])
            if b == 0:
                ends[0, here, :] = whole
            elif b == blocks - 1:
                ends[1, here, :] = whole
            else:
                rounded = whole.astype(BF16)
                mis[b, here, :] = rounded
                row.append((b, rounded))
        sums = 0.0
        for k in range(0, len(row), 2):
            pair = row[k : k + 2]
            left = jnp.concatenate([value for _, value in pair], axis=1)
            first = pair[0][0]
            right = cond[first : first + len(pair)].reshape(len(pair) * width, cond.shape[2])
            sums = sums + dot(left, right)
        part[here, :] = sums

    row_chunks(total, 64, body)


def ends_kernel(dev, load, src, tgt, adm, cond, pair_in, chip_in, ends, part, mis, out):
    blocks, total, width = dev.shape
    edges = src.shape[1]
    last = blocks - 1
    place, count = lax.axis_index("bus"), lax.axis_size("bus")
    even = place % 2 == 0
    ties = jnp.where(even, chip_in[total : total + TIE_ROWS, :].astype(F32), pair_in[total : total + TIE_ROWS, :].astype(F32))

    def twice(row):
        return jnp.concatenate([row[:, 0:edges]] * 2, axis=1)

    src_before = hot_columns(twice(ties[0:1]).astype(I32), width)
    tgt_before = hot_columns(twice(ties[1:2]).astype(I32), width)
    adm_before = twice(ties[2:3] + ties[3:4] + ties[4:5])
    adm_before = jnp.where(place == 0, 0.0, adm_before)
    src_last = hot_columns(twice(src[last : last + 1]), width)
    tgt_last = hot_columns(twice(tgt[last : last + 1]), width)
    adm_last = jnp.where(place == count - 1, 0.0, twice(adm[last : last + 1]))
    right = jnp.concatenate([cond[0], cond[last]], axis=0)

    def body(here):
        pair_rows, chip_rows = pair_in[here, :].astype(F32), chip_in[here, :].astype(F32)
        following = jnp.where(even, pair_rows, chip_rows).astype(BF16)
        leading = jnp.where(even, chip_rows, pair_rows).astype(BF16)
        first = product(dev[0, here, :], load[0, here, :])
        flow_out = adm_last * dot(following, tgt_last)
        flow_in = adm_before * (dot(first, tgt_before) - dot(leading, src_before))
        low = (ends[0, here, :] - dot_t(halves(flow_in, edges), tgt_before)).astype(BF16)
        high = (ends[1, here, :] + dot_t(halves(flow_out, edges), src_last)).astype(BF16)
        mis[0, here, :] = low
        mis[1, here, :] = high
        sums = part[here, :] + dot(jnp.concatenate([low, high], axis=1), right)
        out[here, :] = sums.astype(BF16)

    row_chunks(total, 64, body)


def push_kernel(parts, gain, keep, inner, outer, states, running, sent, mis, sems):
    last = inner.shape[0] - 1
    copies_out = [
        pltpu.make_async_copy(inner.at[pl.ds(1, last - 1)], mis.at[pl.ds(1, last - 1)], sems.at[0]),
        pltpu.make_async_copy(outer.at[0], mis.at[0], sems.at[1]),
        pltpu.make_async_copy(outer.at[1], mis.at[last], sems.at[2]),
    ]
    for copy in copies_out:
        copy.start()
    count, rows, width = parts.shape
    copies = sent.shape[0]

    def add(k, total):
        return total + parts[k].astype(F32)

    section_in = lax.fori_loop(0, count, add, jnp.zeros((rows, width), F32), unroll=8).astype(BF16)
    line = lax.broadcasted_iota(I32, (rows, width), 0)
    pushed = jnp.zeros((rows, width), F32)
    for r in range(rows):
        pushed = jnp.where(line == r, dot(section_in, gain[r]), pushed)
    rate, state = keep[...], pushed
    shift = 1
    while shift < rows:
        reached = line >= shift
        state = state + jnp.where(reached, rate * pltpu.roll(state, shift, 0), 0.0)
        rate = rate * jnp.where(reached, pltpu.roll(rate, shift, 0), 1.0)
        shift *= 2
    states[...] = state
    running[...] = rate
    tiles = width // 128
    lines = [rate[rows - 1 : rows, 128 * k : 128 * k + 128] for k in range(tiles)]
    lines += [state[rows - 1 : rows, 128 * k : 128 * k + 128] for k in range(tiles)]
    both = jnp.concatenate(lines, axis=0)
    for k in range(copies):
        sent[k] = both
    for copy in copies_out:
        copy.wait()


def enter_kernel(spans, states, running, out):
    tiles = spans.shape[1] // 2
    place = lax.axis_index("period") * lax.axis_size("bus") + lax.axis_index("bus")

    def step(k, entering):
        return spans[k, 0:tiles] * entering + spans[k, tiles : 2 * tiles]

    entering = lax.fori_loop(0, place, step, jnp.zeros((tiles, 128), F32))
    flat = jnp.concatenate([entering[k : k + 1] for k in range(tiles)], axis=1)
    out[...] = states[...] + running[...] * flat


def call(kernel, shapes, inputs, scratch=(), specs=None):
    single = not isinstance(shapes, (list, tuple))
    return pl.pallas_call(
        kernel,
        out_shape=shapes,
        in_specs=[VM] * len(inputs),
        out_specs=specs or (VM if single else [VM] * len(shapes)),
        scratch_shapes=list(scratch),
        compiler_params=PARAMS,
    )(*inputs)


def shards(deviation, loading, jacobian, tie_source, tie_target, tie_admittance, condense, section_gain, retention):
    blocks, total, width = deviation.shape
    states_width = condense.shape[2]
    count = lax.axis_size("bus")
    spans = count * lax.axis_size("period")
    rows = section_gain.shape[1]
    shape = jax.ShapeDtypeStruct

    payload = shape((total + TIE_ROWS, width), BF16)
    pair_out, chip_out = call(
        halo_kernel,
        [payload, payload],
        (deviation, loading, tie_source, tie_target, tie_admittance),
        [pltpu.VMEM((TIE_ROWS, width), F32)],
    )
    pairs = [(k, k ^ 1) for k in range(count)]
    chips = [(k, (k + 1) % count if k % 2 else (k - 1) % count) for k in range(count)]
    pair_in = lax.ppermute(pair_out, "bus", pairs)
    chip_in = lax.ppermute(chip_out, "bus", chips)
    inner, ends, part = call(
        inner_kernel,
        [shape((blocks, total, width), BF16), shape((2, total, width), F32), shape((total, states_width), F32)],
        (deviation, loading, jacobian, tie_source, tie_target, tie_admittance, condense),
    )
    outer, sums = call(
        ends_kernel,
        [shape((2, total, width), BF16), shape((total, states_width), BF16)],
        (deviation, loading, tie_source, tie_target, tie_admittance, condense, pair_in, chip_in, ends, part),
    )
    parts = lax.all_to_all(sums.reshape(count, rows, states_width), "bus", 0, 0, tiled=True)
    tiles = 2 * states_width // 128
    states, running, sent, mismatch = call(
        push_kernel,
        [
            shape((rows, states_width), F32),
            shape((rows, states_width), F32),
            shape((spans, tiles, 128), F32),
            shape((blocks, total, width), BF16),
        ],
        (parts, section_gain[0], retention[0], inner, outer),
        [pltpu.SemaphoreType.DMA((3,))],
        [VM, VM, VM, pl.BlockSpec(memory_space=pl.ANY)],
    )
    everything = lax.all_to_all(sent, ("period", "bus"), 0, 0, tiled=True)
    out = call(enter_kernel, shape((rows, states_width), F32), (everything, states, running))
    return (mismatch, out[None])


def solution(mesh):
    placed = (
        P("bus", "period", None),
        P("bus", "period", None),
        P("bus", None, None),
        P("bus", None),
        P("bus", None),
        P("bus", None),
        P("bus", None, None),
        P("period", "bus", None, None),
        P("period", "bus", None),
    )
    return jax.shard_map(
        shards,
        mesh=mesh,
        in_specs=placed,
        out_specs=(P("bus", "period", None), P("period", "bus", None)),
        check_vma=False,
    )
```

time: 107 us -> 37.4 us (0.35)
  blocking collectives: 81.7 us -> 19.4 us
  matrix products: 7.18 us -> 0 us
  Pallas kernels: 0 us -> 3.63 us
  other arithmetic: 3.07 us -> 0 us
  local copies, waits for them, and re-layouts: 7.02 us -> 9.08 us
    all_gather x4 -> x0, blocking collectives: 42 us -> none  [entering_2(): everything = jax.tree.map(lambda part: lax.all_gather(part, axis), value)]
    psum x2 -> x0, blocking collectives: 39.7 us -> none  [the longest x1 26.5 us: shards(): totals = lax.psum(partial_value, 'bus')]
    all_to_all x0 -> x2, blocking collectives: none -> 19.4 us  [the longest x1 12 us: shards(): everything = lax.all_to_all(sent, ('period', 'bus'), 0, 0, tiled=True)]
    unnamed x10 -> x20, local copies, waits for them, and re-layouts: 0.03 us -> 9.08 us
    dot_general x7 -> x0, matrix products: 7.18 us -> none  [the longest x1 2.83 us: shards(): jnp.einsum('tm,tmn->tn', section_in, section_gain[0], preferred_element_t...]
    dynamic_slice x20 -> x0, local copies, waits for them, and re-layouts: 5.96 us -> none  [the longest x8 5.84 us: shards(): lax.scan(advance, (zeros_row, ones_row), (retention[0], pushed))]
    pallas_call x0 -> x5, Pallas kernels: none -> 3.63 us  [call(): pl.pallas_call(kernel, out_shape=shapes, in_specs=[VM] * len(inputs), out...]
    convert_element_type x1 -> x0, other arithmetic: 1.26 us -> none  [shards(): (deviation.astype(jnp.float32) * loading.astype(jnp.float32)).astype(jnp....]
  transfers between devices with their start and end apart: 2 -> 2, of which waited for: 1 -> 0; matrix products, arithmetic and copies ran while one was open for 3% -> 0% of each run, Pallas kernels for 0% -> 3%
where the time goes in v1:
time: 37.4 us; the launch traced here: 36.9 us
  blocking collectives  19.4 us (52%)
  local copies, waits for them, and re-layouts  9.08 us (24%)
  starting transfers between devices  4.07 us (11%)
  Pallas kernels  3.63 us (10%)
  between operations  0.69 us (2%)
    all_to_all x1, blocking collectives, shards(): everything = lax.all_to_all(sent, ('period', 'bus'), 0, 0, tiled=True)  12 us
    unnamed x20, local copies, waits for them, and re-layouts  9.08 us
    all_to_all x1, blocking collectives, shards(): lax.all_to_all(sums.reshape(count, rows, states_width), 'bus', 0, 0, tile...  7.4 us
    pallas_call x5, Pallas kernels, call(): pl.pallas_call(kernel, out_shape=shapes, in_specs=[VM] * len(inputs), out...  3.63 us
    ppermute x1, starting transfers between devices, shards(): chip_in = lax.ppermute(chip_out, 'bus', chips)  3.56 us
  transfers between devices with their start and end apart: 2, of which 0 were waited for; matrix products, arithmetic and copies ran while one was open for 0% of the time, Pallas kernels for 3%

profile of v1, /device:TPU:0, one launch (start us, length us, event | category | flops | bytes accessed | tf_op | source)
XLA Modules:
  0.0 36.9 jit_solution(7188734322039254411)
XLA Ops:
  0.6 0.0 copy-start.3
  0.6 0.9 %copy-done.3 = bf16[16,64,128]{2,1,0:T(8,128)(2,1)S(1)} copy-done((bf16[16,64,128]{2,1,0:T(8,128)(2,1)S(1)}, bf16[16,64,128]{2,1,0:T(8,128)(2,1)}, u32[]{:S(2)}) %copy-start.3) | copy-done | bytes 262168
  1.6 0.0 copy-start.4
  1.6 0.9 %copy-done.4 = bf16[16,64,128]{2,1,0:T(8,128)(2,1)S(1)} copy-done((bf16[16,64,128]{2,1,0:T(8,128)(2,1)S(1)}, bf16[16,64,128]{2,1,0:T(8,128)(2,1)}, u32[]{:S(2)}) %copy-start.4) | copy-done | bytes 262168
  2.5 0.0 copy-start.6
  2.5 0.7 %copy-done.6 = s32[16,16]{1,0:T(8,128)S(1)} copy-done((s32[16,16]{1,0:T(8,128)S(1)}, s32[16,16]{1,0:T(8,128)}, u32[]{:S(2)}) %copy-start.6) | copy-done | bytes 1048
  3.2 0.0 copy-start.7
  3.2 0.7 %copy-done.7 = s32[16,16]{1,0:T(8,128)S(1)} copy-done((s32[16,16]{1,0:T(8,128)S(1)}, s32[16,16]{1,0:T(8,128)}, u32[]{:S(2)}) %copy-start.7) | copy-done | bytes 1048
  3.9 0.0 copy-start.8
  3.9 0.7 %copy-done.8 = f32[16,16]{1,0:T(8,128)S(1)} copy-done((f32[16,16]{1,0:T(8,128)S(1)}, f32[16,16]{1,0:T(8,128)}, u32[]{:S(2)}) %copy-start.8) | copy-done | bytes 1048
  4.6 0.0 copy-start.9
  4.7 0.5 %collective-permute-start = (bf16[80,128]{1,0:T(8,128)(2,1)S(1)}, bf16[80,128]{1,0:T(8,128)(2,1)S(1)}, u32[]{:S(2)}, u32[]{:S(2)}) collective-permute-start(bf16[80,128]{1,0:T(8,128)(2,1)S(1)} %get-tuple-element.13), channel_id=1, source_target_pairs={{0,4},{4,0},{8,12},{12,8},{16,20},{20,16},{24,28},{28,24},{1,5},{5... | collective-permute-start | bytes 61448 | tf_op jit(solution)/shard_map/ppermute | solution.py:239
  5.2 3.6 %collective-permute-start.1 = (bf16[80,128]{1,0:T(8,128)(2,1)S(1)}, bf16[80,128]{1,0:T(8,128)(2,1)S(1)}, u32[]{:S(2)}, u32[]{:S(2)}) collective-permute-start(bf16[80,128]{1,0:T(8,128)(2,1)S(1)} %get-tuple-element.14), channel_id=1, source_target_pairs={{0,28},{4,8},{8,4},{12,16},{16,12},{20,24},{24,20},{28,0},{1,29},{... | collective-permute-start | bytes 61448 | tf_op jit(solution)/shard_map/ppermute | solution.py:240
  8.7 0.0 copy-start
  8.7 1.6 %copy-done = bf16[16,128,512]{2,1,0:T(8,128)(2,1)S(1)} copy-done((bf16[16,128,512]{2,1,0:T(8,128)(2,1)S(1)}, bf16[16,128,512]{2,1,0:T(8,128)(2,1)}, u32[]{:S(2)}) %copy-start) | copy-done | bytes 2097176
  10.3 0.0 copy-start.5
  10.3 1.0 %copy-done.5 = bf16[16,128,128]{2,1,0:T(8,128)(2,1)S(1)} copy-done((bf16[16,128,128]{2,1,0:T(8,128)(2,1)S(1)}, bf16[16,128,128]{2,1,0:T(8,128)(2,1)}, u32[]{:S(2)}) %copy-start.5) | copy-done | bytes 524312
  11.4 0.0 copy-start.1
  11.4 1.3 %shard_map.105 = (bf16[16,64,128]{2,1,0:T(8,128)(2,1)S(1)}, f32[2,64,128]{2,1,0:T(8,128)S(1)}, f32[64,512]{1,0:T(8,128)S(1)}) custom-call(bf16[16,64,128]{2,1,0:T(8,128)(2,1)S(1)} %copy-done.3, bf16[16,64,128]{2,1,0:T(8,128)(2,1)S(1)} %copy-done.4, bf16[16,128,128]{2,1,0:T(8,128)(2,1)S(1)} %copy-done.5, s32[16,16]{1,0:T(8,128)S(1)} %copy-done.6, ...), custom_call_target="tpu_custom_call" | custom-call | tf_op jit(solution)/shard_map/pallas_call | solution.py:212
  12.7 0.0 collective-permute-done.pair_in
  12.7 0.0 collective-permute-done.1.chip_in
  12.7 0.3 copy-done.1
  13.0 0.5 %shard_map.106 = (bf16[2,64,128]{2,1,0:T(8,128)(2,1)S(1)}, bf16[64,512]{1,0:T(8,128)(2,1)S(1)}) custom-call(bf16[16,64,128]{2,1,0:T(8,128)(2,1)S(1)} %copy-done.3, bf16[16,64,128]{2,1,0:T(8,128)(2,1)S(1)} %copy-done.4, s32[16,16]{1,0:T(8,128)S(1)} %copy-done.6, s32[16,16]{1,0:T(8,128)S(1)} %copy-done.7, f32[16,16]{1,0:T(8,128)S(1)} %copy-done.8, ...), custom_call_target="tpu_custom_call" | custom-call | tf_op jit(solution)/shard_map/pallas_call | solution.py:212
  13.4 7.4 %all_to_all.10.parts = bf16[8,8,512]{2,1,0:T(8,128)(2,1)S(1)} all-to-all(bf16[8,8,512]{2,1,0:T(8,128)(2,1)S(1)} %bitcast.5), channel_id=1, replica_groups=mesh['bus'=8,'period'=4] {'bus'}, dimensions={0} | all-to-all | bytes 131072 | tf_op jit(solution)/shard_map/all_to_all | solution.py:251
  20.8 0.0 copy-done.9
  20.8 0.0 copy-start.2
  20.8 2.2 %copy-done.2 = bf16[1,8,512,512]{3,2,1,0:T(8,128)(2,1)S(1)} copy-done((bf16[1,8,512,512]{3,2,1,0:T(8,128)(2,1)S(1)}, bf16[1,8,512,512]{3,2,1,0:T(8,128)(2,1)}, u32[]{:S(2)}) %copy-start.2) | copy-done | bytes 4194328
  23.0 1.2 %shard_map.107 = (f32[8,512]{1,0:T(8,128)S(1)}, f32[8,512]{1,0:T(8,128)S(1)}, f32[32,8,128]{2,1,0:T(8,128)S(1)}, bf16[16,64,128]{2,1,0:T(8,128)(2,1)}) custom-call(bf16[8,8,512]{2,1,0:T(8,128)(2,1)S(1)} %all_to_all.10.parts, bf16[8,512,512]{2,1,0:T(8,128)(2,1)S(1)} %bitcast.4, f32[8,512]{1,0:T(8,128)S(1)} %bitcast.6, ...), custom_call_target="tpu_custom_call" | custom-call | tf_op jit(solution)/shard_map/pallas_call | solution.py:212
  24.3 12.0 %all_to_all.11.spans = f32[32,8,128]{2,1,0:T(8,128)S(1)} all-to-all(f32[32,8,128]{2,1,0:T(8,128)S(1)} %get-tuple-element.21), channel_id=1, replica_groups=mesh['bus'=8,'period'=4] {'period','bus'}, dimensions={0} | all-to-all | bytes 262144 | tf_op jit(solution)/shard_map/all_to_all | solution.py:265
  36.3 0.6 %shard_map.108 = f32[8,512]{1,0:T(8,128)} custom-call(f32[32,8,128]{2,1,0:T(8,128)S(1)} %all_to_all.11.spans, f32[8,512]{1,0:T(8,128)S(1)} %get-tuple-element.22.states, f32[8,512]{1,0:T(8,128)S(1)} %get-tuple-element.23.running), custom_call_target="tpu_custom_call" | custom-call | tf_op jit(solution)/shard_map/pallas_call | solution.py:212
  (1 shorter events, 0.0 us)
Async XLA Ops:
  0.6 1.0 %copy-start.3 = (bf16[16,64,128]{2,1,0:T(8,128)(2,1)S(1)}, bf16[16,64,128]{2,1,0:T(8,128)(2,1)}, u32[]{:S(2)}) copy-start(bf16[16,64,128]{2,1,0:T(8,128)(2,1)} %dev.5) | copy-start | bytes 786436
  1.6 0.9 %copy-start.4 = (bf16[16,64,128]{2,1,0:T(8,128)(2,1)S(1)}, bf16[16,64,128]{2,1,0:T(8,128)(2,1)}, u32[]{:S(2)}) copy-start(bf16[16,64,128]{2,1,0:T(8,128)(2,1)} %load.5) | copy-start | bytes 786436
  2.5 0.7 %copy-start.6 = (s32[16,16]{1,0:T(8,128)S(1)}, s32[16,16]{1,0:T(8,128)}, u32[]{:S(2)}) copy-start(s32[16,16]{1,0:T(8,128)} %src.5) | copy-start | bytes 3076
  3.2 0.7 %copy-start.7 = (s32[16,16]{1,0:T(8,128)S(1)}, s32[16,16]{1,0:T(8,128)}, u32[]{:S(2)}) copy-start(s32[16,16]{1,0:T(8,128)} %tgt.5) | copy-start | bytes 3076
  3.9 0.7 %copy-start.8 = (f32[16,16]{1,0:T(8,128)S(1)}, f32[16,16]{1,0:T(8,128)}, u32[]{:S(2)}) copy-start(f32[16,16]{1,0:T(8,128)} %adm.5) | copy-start | bytes 3076
  4.6 16.2 %copy-start.9 = (f32[1,8,512]{2,1,0:T(8,128)S(1)}, f32[1,8,512]{2,1,0:T(8,128)}, u32[]{:S(2)}) copy-start(f32[1,8,512]{2,1,0:T(8,128)} %param.17) | copy-start | bytes 49156
  4.7 8.0 %collective-permute-start = (bf16[80,128]{1,0:T(8,128)(2,1)S(1)}, bf16[80,128]{1,0:T(8,128)(2,1)S(1)}, u32[]{:S(2)}, u32[]{:S(2)}) collective-permute-start(bf16[80,128]{1,0:T(8,128)(2,1)S(1)} %get-tuple-element.13), channel_id=1, source_target_pairs={{0,4},{4,0},{8,12},{12,8},{16,20},{20,16},{24,28},{28,24},{1,5},{5... | collective-permute-start | bytes 61448 | tf_op jit(solution)/shard_map/ppermute | solution.py:239
  5.2 7.5 %collective-permute-start.1 = (bf16[80,128]{1,0:T(8,128)(2,1)S(1)}, bf16[80,128]{1,0:T(8,128)(2,1)S(1)}, u32[]{:S(2)}, u32[]{:S(2)}) collective-permute-start(bf16[80,128]{1,0:T(8,128)(2,1)S(1)} %get-tuple-element.14), channel_id=1, source_target_pairs={{0,28},{4,8},{8,4},{12,16},{16,12},{20,24},{24,20},{28,0},{1,29},{... | collective-permute-start | bytes 61448 | tf_op jit(solution)/shard_map/ppermute | solution.py:240
  8.7 1.6 %copy-start = (bf16[16,128,512]{2,1,0:T(8,128)(2,1)S(1)}, bf16[16,128,512]{2,1,0:T(8,128)(2,1)}, u32[]{:S(2)}) copy-start(bf16[16,128,512]{2,1,0:T(8,128)(2,1)} %cond.3) | copy-start | bytes 6291460
  10.3 1.0 %copy-start.5 = (bf16[16,128,128]{2,1,0:T(8,128)(2,1)S(1)}, bf16[16,128,128]{2,1,0:T(8,128)(2,1)}, u32[]{:S(2)}) copy-start(bf16[16,128,128]{2,1,0:T(8,128)(2,1)} %jac.1) | copy-start | bytes 1572868
  11.4 1.6 %copy-start.1 = (bf16[16,128,512]{2,1,0:T(8,128)(2,1)S(1)}, bf16[16,128,512]{2,1,0:T(8,128)(2,1)}, u32[]{:S(2)}) copy-start(bf16[16,128,512]{2,1,0:T(8,128)(2,1)} %cond.3) | copy-start | bytes 6291460
  20.8 2.2 %copy-start.2 = (bf16[1,8,512,512]{3,2,1,0:T(8,128)(2,1)S(1)}, bf16[1,8,512,512]{3,2,1,0:T(8,128)(2,1)}, u32[]{:S(2)}) copy-start(bf16[1,8,512,512]{3,2,1,0:T(8,128)(2,1)} %param.16) | copy-start | bytes 12582916

commit v2 on v1

--- a/solution.py
+++ b/solution.py
@@ -8,7 +8,8 @@
 F32, BF16, I32 = jnp.float32, jnp.bfloat16, jnp.int32
 VM = pl.BlockSpec(memory_space=pltpu.VMEM)
 TIE_ROWS = 16
-PARAMS = pltpu.CompilerParams(vmem_limit_bytes=48 * 1024 * 1024)
+PARAMS = pltpu.CompilerParams(vmem_limit_bytes=16 * 1024 * 1024)
+HBM = pl.BlockSpec(memory_space=pltpu.HBM)
 
 
 def dot(a, b):
@@ -44,12 +45,30 @@
         body(pl.ds(pl.multiple_of(k * size, size), size))
 
 
-def halo_kernel(dev, load, src, tgt, adm, pair_out, chip_out, ties):
-    blocks, rows, _ = dev.shape
+def halo_kernel(dev_hbm, load_hbm, src_hbm, tgt_hbm, adm_hbm, pair_out, chip_out, dev, load, src, tgt, adm, ties, sems):
+    last = dev_hbm.shape[0] - 1
+    rows = dev.shape[1]
     edges = src.shape[1]
-    last = blocks - 1
+    fetches = [
+        pltpu.make_async_copy(source, target, sems.at[k])
+        for k, (source, target) in enumerate(
+            [
+                (dev_hbm.at[0], dev.at[0]),
+                (dev_hbm.at[last], dev.at[1]),
+                (load_hbm.at[0], load.at[0]),
+                (load_hbm.at[last], load.at[1]),
+                (src_hbm, src),
+                (tgt_hbm, tgt),
+                (adm_hbm, adm),
+            ]
+        )
+    ]
+    for fetch in fetches:
+        fetch.start()
     even = lax.axis_index("bus") % 2 == 0
     ties[...] = jnp.zeros_like(ties)
+    for fetch in fetches:
+        fetch.wait()
     a = adm[last : last + 1, :]
     high = a.astype(BF16).astype(F32)
     mid = (a - high).astype(BF16).astype(F32)
@@ -60,16 +79,9 @@
     ties[4:5, 0:edges] = a - high - mid
     packed = ties[...].astype(BF16)
 
-    @pl.when(even)
-    def _():
-        pair_out[0:rows, :] = product(dev[last], load[last])
-        chip_out[0:rows, :] = product(dev[0], load[0])
-
-    @pl.when(jnp.logical_not(even))
-    def _():
-        pair_out[0:rows, :] = product(dev[0], load[0])
-        chip_out[0:rows, :] = product(dev[last], load[last])
-
+    first, final = product(dev[0], load[0]).astype(F32), product(dev[1], load[1]).astype(F32)
+    pair_out[0:rows, :] = jnp.where(even, final, first).astype(BF16)
+    chip_out[0:rows, :] = jnp.where(even, first, final).astype(BF16)
     pair_out[rows : rows + TIE_ROWS, :] = packed
     chip_out[rows : rows + TIE_ROWS, :] = packed
 
@@ -207,21 +219,22 @@
     out[...] = states[...] + running[...] * flat
 
 
-def call(kernel, shapes, inputs, scratch=(), specs=None):
+def call(kernel, shapes, inputs, cost, scratch=(), specs=None, ins=None):
     single = not isinstance(shapes, (list, tuple))
     return pl.pallas_call(
         kernel,
         out_shape=shapes,
-        in_specs=[VM] * len(inputs),
+        in_specs=ins or [VM] * len(inputs),
         out_specs=specs or (VM if single else [VM] * len(shapes)),
         scratch_shapes=list(scratch),
         compiler_params=PARAMS,
+        cost_estimate=pl.CostEstimate(flops=int(cost * 1e9), transcendentals=0, bytes_accessed=int(cost * 3.0e6)),
     )(*inputs)
 
 
 def shards(deviation, loading, jacobian, tie_source, tie_target, tie_admittance, condense, section_gain, retention):
     blocks, total, width = deviation.shape
-    states_width = condense.shape[2]
+    states_width, edges = condense.shape[2], tie_source.shape[1]
     count = lax.axis_size("bus")
     spans = count * lax.axis_size("period")
     rows = section_gain.shape[1]
@@ -231,8 +244,18 @@
     pair_out, chip_out = call(
         halo_kernel,
         [payload, payload],
-        (deviation, loading, tie_source, tie_target, tie_admittance),
-        [pltpu.VMEM((TIE_ROWS, width), F32)],
+        [pltpu.with_memory_space_constraint(x, pltpu.HBM) for x in (deviation, loading, tie_source, tie_target, tie_admittance)],
+        10.0,
+        [
+            pltpu.VMEM((2, total, width), BF16),
+            pltpu.VMEM((2, total, width), BF16),
+            pltpu.VMEM((blocks, edges), I32),
+            pltpu.VMEM((blocks, edges), I32),
+            pltpu.VMEM((blocks, edges), F32),
+            pltpu.VMEM((TIE_ROWS, width), F32),
+            pltpu.SemaphoreType.DMA((7,)),
+        ],
+        ins=[HBM] * 5,
     )
     pairs = [(k, k ^ 1) for k in range(count)]
     chips = [(k, (k + 1) % count if k % 2 else (k - 1) % count) for k in range(count)]
@@ -242,11 +265,13 @@
         inner_kernel,
         [shape((blocks, total, width), BF16), shape((2, total, width), F32), shape((total, states_width), F32)],
         (deviation, loading, jacobian, tie_source, tie_target, tie_admittance, condense),
+        5.0,
     )
     outer, sums = call(
         ends_kernel,
         [shape((2, total, width), BF16), shape((total, states_width), BF16)],
         (deviation, loading, tie_source, tie_target, tie_admittance, condense, pair_in, chip_in, ends, part),
+        1.0,
     )
     parts = lax.all_to_all(sums.reshape(count, rows, states_width), "bus", 0, 0, tiled=True)
     tiles = 2 * states_width // 128
@@ -259,11 +284,12 @@
             shape((blocks, total, width), BF16),
         ],
         (parts, section_gain[0], retention[0], inner, outer),
+        2.0,
         [pltpu.SemaphoreType.DMA((3,))],
-        [VM, VM, VM, pl.BlockSpec(memory_space=pl.ANY)],
+        [VM, VM, VM, HBM],
     )
     everything = lax.all_to_all(sent, ("period", "bus"), 0, 0, tiled=True)
-    out = call(enter_kernel, shape((rows, states_width), F32), (everything, states, running))
+    out = call(enter_kernel, shape((rows, states_width), F32), (everything, states, running), 1.0)
     return (mismatch, out[None])
 
 

time: 37.4 us -> 30.6 us (0.82)
  local copies, waits for them, and re-layouts: 9.08 us -> 0.04 us
  blocking collectives: 19.4 us -> 20.7 us
  Pallas kernels: 3.63 us -> 4.61 us
    unnamed x20 -> x18, local copies, waits for them, and re-layouts: 9.08 us -> 0.04 us
    all_to_all x1, blocking collectives: 7.4 us -> 8.72 us  [shards(): lax.all_to_all(sums.reshape(count, rows, states_width), 'bus', 0, 0, tile...]
    pallas_call x5, Pallas kernels: 3.63 us -> 4.61 us  [call(): pl.pallas_call(kernel, out_shape=shapes, in_specs=ins or [VM] * len(input...]
  transfers between devices with their start and end apart: 2 -> 2, of which waited for: 0 -> 1; matrix products, arithmetic and copies ran while one was open for 0% -> 0% of each run, Pallas kernels for 3% -> 4%
where the time goes in v2:
time: 30.6 us; the launch traced here: 30.3 us
  blocking collectives  20.7 us (68%)
  Pallas kernels  4.61 us (15%)
  starting transfers between devices  4.07 us (13%)
  between operations  0.75 us (2%)
    all_to_all x1, blocking collectives, shards(): everything = lax.all_to_all(sent, ('period', 'bus'), 0, 0, tiled=True)  12 us
    all_to_all x1, blocking collectives, shards(): lax.all_to_all(sums.reshape(count, rows, states_width), 'bus', 0, 0, tile...  8.72 us
    pallas_call x5, Pallas kernels, call(): pl.pallas_call(kernel, out_shape=shapes, in_specs=ins or [VM] * len(input...  4.61 us
    ppermute x1, starting transfers between devices, shards(): chip_in = lax.ppermute(chip_out, 'bus', chips)  3.56 us
  transfers between devices with their start and end apart: 2, of which 1 were waited for; matrix products, arithmetic and copies ran while one was open for 0% of the time, Pallas kernels for 4%

profile of v2, /device:TPU:0, one launch (start us, length us, event | category | flops | bytes accessed | tf_op | source)
XLA Modules:
  0.0 30.3 jit_solution(17575371800299470956)
XLA Ops:
  0.6 0.0 copy-start.8
  0.6 0.0 copy-start.7
  0.7 0.0 copy-start.6
  0.7 0.0 copy-start.4
  0.7 0.0 copy-start.3
  0.7 0.0 copy-start.1
  0.7 0.0 copy-start.2
  0.7 1.0 %shard_map.104 = (bf16[80,128]{1,0:T(8,128)(2,1)S(1)}, bf16[80,128]{1,0:T(8,128)(2,1)S(1)}) custom-call(bf16[16,64,128]{2,1,0:T(8,128)(2,1)} %dev.3, bf16[16,64,128]{2,1,0:T(8,128)(2,1)} %load.3, s32[16,16]{1,0:T(8,128)} %src.3, s32[16,16]{1,0:T(8,128)} %tgt.3, f32[16,16]{1,0:T(8,128)} %adm.3), custom_call_target="tpu_custom_call" | custom-call | flops 10000000000 | bytes 30000000 | tf_op jit(solution)/shard_map/pallas_call | solution.py:224
  1.7 0.5 %collective-permute-start = (bf16[80,128]{1,0:T(8,128)(2,1)S(1)}, bf16[80,128]{1,0:T(8,128)(2,1)S(1)}, u32[]{:S(2)}, u32[]{:S(2)}) collective-permute-start(bf16[80,128]{1,0:T(8,128)(2,1)S(1)} %get-tuple-element.13), channel_id=1, source_target_pairs={{0,4},{4,0},{8,12},{12,8},{16,20},{20,16},{24,28},{28,24},{1,5},{5... | collective-permute-start | bytes 61448 | tf_op jit(solution)/shard_map/ppermute | solution.py:262
  2.2 0.0 copy-start
  2.2 0.0 copy-start.5
  2.2 3.6 %collective-permute-start.1 = (bf16[80,128]{1,0:T(8,128)(2,1)S(1)}, bf16[80,128]{1,0:T(8,128)(2,1)S(1)}, u32[]{:S(2)}, u32[]{:S(2)}) collective-permute-start(bf16[80,128]{1,0:T(8,128)(2,1)S(1)} %get-tuple-element.14), channel_id=1, source_target_pairs={{0,28},{4,8},{8,4},{12,16},{16,12},{20,24},{24,20},{28,0},{1,29},{... | collective-permute-start | bytes 61448 | tf_op jit(solution)/shard_map/ppermute | solution.py:263
  5.8 0.0 copy-done.8
  5.8 0.0 copy-done.7
  5.8 0.0 copy-done.6
  5.8 0.0 copy-done.4
  5.8 0.0 copy-done.3
  5.8 0.0 copy-done.1
  5.8 0.0 copy-done.2
  5.8 1.3 %shard_map.105 = (bf16[16,64,128]{2,1,0:T(8,128)(2,1)S(1)}, f32[2,64,128]{2,1,0:T(8,128)S(1)}, f32[64,512]{1,0:T(8,128)S(1)}) custom-call(bf16[16,64,128]{2,1,0:T(8,128)(2,1)S(1)} %copy-done.3, bf16[16,64,128]{2,1,0:T(8,128)(2,1)S(1)} %copy-done.4, bf16[16,128,128]{2,1,0:T(8,128)(2,1)S(1)} %copy-done.2, s32[16,16]{1,0:T(8,128)S(1)} %copy-done.6, ...), custom_call_target="tpu_custom_call" | custom-call | flops 5000000000 | bytes 15000000 | tf_op jit(solution)/shard_map/pallas_call | solution.py:224
  7.1 0.0 collective-permute-done.pair_in
  7.1 0.1 collective-permute-done.1.chip_in
  7.3 0.5 %shard_map.106 = (bf16[2,64,128]{2,1,0:T(8,128)(2,1)S(1)}, bf16[64,512]{1,0:T(8,128)(2,1)S(1)}) custom-call(bf16[16,64,128]{2,1,0:T(8,128)(2,1)S(1)} %copy-done.3, bf16[16,64,128]{2,1,0:T(8,128)(2,1)S(1)} %copy-done.4, s32[16,16]{1,0:T(8,128)S(1)} %copy-done.6, s32[16,16]{1,0:T(8,128)S(1)} %copy-done.7, f32[16,16]{1,0:T(8,128)S(1)} %copy-done.8, ...), custom_call_target="tpu_custom_call" | custom-call | flops 1000000000 | bytes 3000000 | tf_op jit(solution)/shard_map/pallas_call | solution.py:224
  7.7 8.7 %all_to_all.10.parts = bf16[8,8,512]{2,1,0:T(8,128)(2,1)S(1)} all-to-all(bf16[8,8,512]{2,1,0:T(8,128)(2,1)S(1)} %bitcast.4), channel_id=1, replica_groups=mesh['bus'=8,'period'=4] {'bus'}, dimensions={0} | all-to-all | bytes 131072 | tf_op jit(solution)/shard_map/all_to_all | solution.py:276
  16.5 0.0 copy-done
  16.5 0.0 copy-done.5
  16.5 1.2 %shard_map.107 = (f32[8,512]{1,0:T(8,128)S(1)}, f32[8,512]{1,0:T(8,128)S(1)}, f32[32,8,128]{2,1,0:T(8,128)S(1)}, bf16[16,64,128]{2,1,0:T(8,128)(2,1)}) custom-call(bf16[8,8,512]{2,1,0:T(8,128)(2,1)S(1)} %all_to_all.10.parts, bf16[8,512,512]{2,1,0:T(8,128)(2,1)S(1)} %bitcast.5, f32[8,512]{1,0:T(8,128)S(1)} %bitcast.6, ...), custom_call_target="tpu_custom_call" | custom-call | flops 2000000000 | bytes 6000000 | tf_op jit(solution)/shard_map/pallas_call | solution.py:224
  17.7 12.0 %all_to_all.11.spans = f32[32,8,128]{2,1,0:T(8,128)S(1)} all-to-all(f32[32,8,128]{2,1,0:T(8,128)S(1)} %get-tuple-element.21), channel_id=1, replica_groups=mesh['bus'=8,'period'=4] {'period','bus'}, dimensions={0} | all-to-all | bytes 262144 | tf_op jit(solution)/shard_map/all_to_all | solution.py:291
  29.7 0.6 %shard_map.108 = f32[8,512]{1,0:T(8,128)} custom-call(f32[32,8,128]{2,1,0:T(8,128)S(1)} %all_to_all.11.spans, f32[8,512]{1,0:T(8,128)S(1)} %get-tuple-element.22.states, f32[8,512]{1,0:T(8,128)S(1)} %get-tuple-element.23.running), custom_call_target="tpu_custom_call" | custom-call | flops 1000000000 | bytes 3000000 | tf_op jit(solution)/shard_map/pallas_call | solution.py:224
Async XLA Ops:
  0.6 5.2 %copy-start.8 = (f32[16,16]{1,0:T(8,128)S(1)}, f32[16,16]{1,0:T(8,128)}, u32[]{:S(2)}) copy-start(f32[16,16]{1,0:T(8,128)} %adm.3) | copy-start | bytes 3076
  0.6 5.2 %copy-start.7 = (s32[16,16]{1,0:T(8,128)S(1)}, s32[16,16]{1,0:T(8,128)}, u32[]{:S(2)}) copy-start(s32[16,16]{1,0:T(8,128)} %tgt.3) | copy-start | bytes 3076
  0.7 5.1 %copy-start.6 = (s32[16,16]{1,0:T(8,128)S(1)}, s32[16,16]{1,0:T(8,128)}, u32[]{:S(2)}) copy-start(s32[16,16]{1,0:T(8,128)} %src.3) | copy-start | bytes 3076
  0.7 5.1 %copy-start.4 = (bf16[16,64,128]{2,1,0:T(8,128)(2,1)S(1)}, bf16[16,64,128]{2,1,0:T(8,128)(2,1)}, u32[]{:S(2)}) copy-start(bf16[16,64,128]{2,1,0:T(8,128)(2,1)} %load.3) | copy-start | bytes 786436
  0.7 5.1 %copy-start.3 = (bf16[16,64,128]{2,1,0:T(8,128)(2,1)S(1)}, bf16[16,64,128]{2,1,0:T(8,128)(2,1)}, u32[]{:S(2)}) copy-start(bf16[16,64,128]{2,1,0:T(8,128)(2,1)} %dev.3) | copy-start | bytes 786436
  0.7 5.1 %copy-start.1 = (bf16[16,128,512]{2,1,0:T(8,128)(2,1)S(1)}, bf16[16,128,512]{2,1,0:T(8,128)(2,1)}, u32[]{:S(2)}) copy-start(bf16[16,128,512]{2,1,0:T(8,128)(2,1)} %cond.3) | copy-start | bytes 6291460
  0.7 5.1 %copy-start.2 = (bf16[16,128,128]{2,1,0:T(8,128)(2,1)S(1)}, bf16[16,128,128]{2,1,0:T(8,128)(2,1)}, u32[]{:S(2)}) copy-start(bf16[16,128,128]{2,1,0:T(8,128)(2,1)} %jac.1) | copy-start | bytes 1572868
  1.7 5.4 %collective-permute-start = (bf16[80,128]{1,0:T(8,128)(2,1)S(1)}, bf16[80,128]{1,0:T(8,128)(2,1)S(1)}, u32[]{:S(2)}, u32[]{:S(2)}) collective-permute-start(bf16[80,128]{1,0:T(8,128)(2,1)S(1)} %get-tuple-element.13), channel_id=1, source_target_pairs={{0,4},{4,0},{8,12},{12,8},{16,20},{20,16},{24,28},{28,24},{1,5},{5... | collective-permute-start | bytes 61448 | tf_op jit(solution)/shard_map/ppermute | solution.py:262
  2.2 14.2 %copy-start = (bf16[1,8,512,512]{3,2,1,0:T(8,128)(2,1)S(1)}, bf16[1,8,512,512]{3,2,1,0:T(8,128)(2,1)}, u32[]{:S(2)}) copy-start(bf16[1,8,512,512]{3,2,1,0:T(8,128)(2,1)} %param.16) | copy-start | bytes 12582916
  2.2 14.2 %copy-start.5 = (f32[1,8,512]{2,1,0:T(8,128)S(1)}, f32[1,8,512]{2,1,0:T(8,128)}, u32[]{:S(2)}) copy-start(f32[1,8,512]{2,1,0:T(8,128)} %param.17) | copy-start | bytes 49156
  2.2 5.0 %collective-permute-start.1 = (bf16[80,128]{1,0:T(8,128)(2,1)S(1)}, bf16[80,128]{1,0:T(8,128)(2,1)S(1)}, u32[]{:S(2)}, u32[]{:S(2)}) collective-permute-start(bf16[80,128]{1,0:T(8,128)(2,1)S(1)} %get-tuple-element.14), channel_id=1, source_target_pairs={{0,28},{4,8},{8,4},{12,16},{16,12},{20,24},{24,20},{28,0},{1,29},{... | collective-permute-start | bytes 61448 | tf_op jit(solution)/shard_map/ppermute | solution.py:263

commit v3 on v2

--- a/solution.py
+++ b/solution.py
@@ -131,7 +131,7 @@
     row_chunks(total, 64, body)
 
 
-def ends_kernel(dev, load, src, tgt, adm, cond, pair_in, chip_in, ends, part, mis, out):
+def ends_kernel(dev, load, src, tgt, adm, cond, chip_in, pair_in, ends, part, mis, out):
     blocks, total, width = dev.shape
     edges = src.shape[1]
     last = blocks - 1
@@ -259,8 +259,8 @@
     )
     pairs = [(k, k ^ 1) for k in range(count)]
     chips = [(k, (k + 1) % count if k % 2 else (k - 1) % count) for k in range(count)]
+    chip_in = lax.ppermute(chip_out, "bus", chips)
     pair_in = lax.ppermute(pair_out, "bus", pairs)
-    chip_in = lax.ppermute(chip_out, "bus", chips)
     inner, ends, part = call(
         inner_kernel,
         [shape((blocks, total, width), BF16), shape((2, total, width), F32), shape((total, states_width), F32)],
@@ -270,7 +270,7 @@
     outer, sums = call(
         ends_kernel,
         [shape((2, total, width), BF16), shape((total, states_width), BF16)],
-        (deviation, loading, tie_source, tie_target, tie_admittance, condense, pair_in, chip_in, ends, part),
+        (deviation, loading, tie_source, tie_target, tie_admittance, condense, chip_in, pair_in, ends, part),
         1.0,
     )
     parts = lax.all_to_all(sums.reshape(count, rows, states_width), "bus", 0, 0, tiled=True)

time: 30.6 us -> 29.9 us (0.977)
  starting transfers between devices: 4.07 us -> 3.4 us
    ppermute x1, starting transfers between devices: 0.52 us -> 0.01 us  [shards(): pair_in = lax.ppermute(pair_out, 'bus', pairs)]
where the time goes in v3:
time: 29.9 us; the launch traced here: 29.7 us
  blocking collectives  20.7 us (69%)
  Pallas kernels  4.61 us (15%)
  starting transfers between devices  3.4 us (11%)
  between operations  0.77 us (3%)
    all_to_all x1, blocking collectives, shards(): everything = lax.all_to_all(sent, ('period', 'bus'), 0, 0, tiled=True)  12 us
    all_to_all x1, blocking collectives, shards(): lax.all_to_all(sums.reshape(count, rows, states_width), 'bus', 0, 0, tile...  8.72 us
    pallas_call x5, Pallas kernels, call(): pl.pallas_call(kernel, out_shape=shapes, in_specs=ins or [VM] * len(input...  4.61 us
    ppermute x1, starting transfers between devices, shards(): chip_in = lax.ppermute(chip_out, 'bus', chips)  3.4 us
  transfers between devices with their start and end apart: 2, of which 1 were waited for; matrix products, arithmetic and copies ran while one was open for 0% of the time, Pallas kernels for 4%

profile of v3, /device:TPU:0, one launch (start us, length us, event | category | flops | bytes accessed | tf_op | source)
XLA Modules:
  0.0 29.7 jit_solution(11197823315626740793)
XLA Ops:
  0.6 0.0 copy-start.8
  0.6 0.0 copy-start.7
  0.7 0.0 copy-start.6
  0.7 0.0 copy-start.4
  0.7 0.0 copy-start.3
  0.7 0.0 copy-start.1
  0.7 0.0 copy-start.2
  0.7 1.0 %shard_map.104 = (bf16[80,128]{1,0:T(8,128)(2,1)S(1)}, bf16[80,128]{1,0:T(8,128)(2,1)S(1)}) custom-call(bf16[16,64,128]{2,1,0:T(8,128)(2,1)} %dev.3, bf16[16,64,128]{2,1,0:T(8,128)(2,1)} %load.3, s32[16,16]{1,0:T(8,128)} %src.3, s32[16,16]{1,0:T(8,128)} %tgt.3, f32[16,16]{1,0:T(8,128)} %adm.3), custom_call_target="tpu_custom_call" | custom-call | flops 10000000000 | bytes 30000000 | tf_op jit(solution)/shard_map/pallas_call | solution.py:224
  1.7 3.4 %collective-permute-start = (bf16[80,128]{1,0:T(8,128)(2,1)S(1)}, bf16[80,128]{1,0:T(8,128)(2,1)S(1)}, u32[]{:S(2)}, u32[]{:S(2)}) collective-permute-start(bf16[80,128]{1,0:T(8,128)(2,1)S(1)} %get-tuple-element.13), channel_id=1, source_target_pairs={{0,28},{4,8},{8,4},{12,16},{16,12},{20,24},{24,20},{28,0},{1,29},{... | collective-permute-start | bytes 61448 | tf_op jit(solution)/shard_map/ppermute | solution.py:262
  5.1 0.0 copy-start
  5.1 0.0 copy-start.5
  5.1 0.0 collective-permute-start.1
  5.1 0.0 copy-done.8
  5.1 0.0 copy-done.7
  5.1 0.0 copy-done.6
  5.1 0.0 copy-done.4
  5.1 0.0 copy-done.3
  5.2 0.0 copy-done.1
  5.2 0.0 copy-done.2
  5.2 1.3 %shard_map.105 = (bf16[16,64,128]{2,1,0:T(8,128)(2,1)S(1)}, f32[2,64,128]{2,1,0:T(8,128)S(1)}, f32[64,512]{1,0:T(8,128)S(1)}) custom-call(bf16[16,64,128]{2,1,0:T(8,128)(2,1)S(1)} %copy-done.3, bf16[16,64,128]{2,1,0:T(8,128)(2,1)S(1)} %copy-done.4, bf16[16,128,128]{2,1,0:T(8,128)(2,1)S(1)} %copy-done.2, s32[16,16]{1,0:T(8,128)S(1)} %copy-done.6, ...), custom_call_target="tpu_custom_call" | custom-call | flops 5000000000 | bytes 15000000 | tf_op jit(solution)/shard_map/pallas_call | solution.py:224
  6.5 0.1 collective-permute-done.chip_in
  6.6 0.0 collective-permute-done.1.pair_in
  6.6 0.5 %shard_map.106 = (bf16[2,64,128]{2,1,0:T(8,128)(2,1)S(1)}, bf16[64,512]{1,0:T(8,128)(2,1)S(1)}) custom-call(bf16[16,64,128]{2,1,0:T(8,128)(2,1)S(1)} %copy-done.3, bf16[16,64,128]{2,1,0:T(8,128)(2,1)S(1)} %copy-done.4, s32[16,16]{1,0:T(8,128)S(1)} %copy-done.6, s32[16,16]{1,0:T(8,128)S(1)} %copy-done.7, f32[16,16]{1,0:T(8,128)S(1)} %copy-done.8, ...), custom_call_target="tpu_custom_call" | custom-call | flops 1000000000 | bytes 3000000 | tf_op jit(solution)/shard_map/pallas_call | solution.py:224
  7.1 8.7 %all_to_all.10.parts = bf16[8,8,512]{2,1,0:T(8,128)(2,1)S(1)} all-to-all(bf16[8,8,512]{2,1,0:T(8,128)(2,1)S(1)} %bitcast.4), channel_id=1, replica_groups=mesh['bus'=8,'period'=4] {'bus'}, dimensions={0} | all-to-all | bytes 131072 | tf_op jit(solution)/shard_map/all_to_all | solution.py:276
  15.8 0.0 copy-done
  15.8 0.0 copy-done.5
  15.8 1.2 %shard_map.107 = (f32[8,512]{1,0:T(8,128)S(1)}, f32[8,512]{1,0:T(8,128)S(1)}, f32[32,8,128]{2,1,0:T(8,128)S(1)}, bf16[16,64,128]{2,1,0:T(8,128)(2,1)}) custom-call(bf16[8,8,512]{2,1,0:T(8,128)(2,1)S(1)} %all_to_all.10.parts, bf16[8,512,512]{2,1,0:T(8,128)(2,1)S(1)} %bitcast.5, f32[8,512]{1,0:T(8,128)S(1)} %bitcast.6, ...), custom_call_target="tpu_custom_call" | custom-call | flops 2000000000 | bytes 6000000 | tf_op jit(solution)/shard_map/pallas_call | solution.py:224
  17.0 12.0 %all_to_all.11.spans = f32[32,8,128]{2,1,0:T(8,128)S(1)} all-to-all(f32[32,8,128]{2,1,0:T(8,128)S(1)} %get-tuple-element.21), channel_id=1, replica_groups=mesh['bus'=8,'period'=4] {'period','bus'}, dimensions={0} | all-to-all | bytes 262144 | tf_op jit(solution)/shard_map/all_to_all | solution.py:291
  29.0 0.6 %shard_map.108 = f32[8,512]{1,0:T(8,128)} custom-call(f32[32,8,128]{2,1,0:T(8,128)S(1)} %all_to_all.11.spans, f32[8,512]{1,0:T(8,128)S(1)} %get-tuple-element.22.states, f32[8,512]{1,0:T(8,128)S(1)} %get-tuple-element.23.running), custom_call_target="tpu_custom_call" | custom-call | flops 1000000000 | bytes 3000000 | tf_op jit(solution)/shard_map/pallas_call | solution.py:224
Async XLA Ops:
  0.6 4.5 %copy-start.8 = (f32[16,16]{1,0:T(8,128)S(1)}, f32[16,16]{1,0:T(8,128)}, u32[]{:S(2)}) copy-start(f32[16,16]{1,0:T(8,128)} %adm.3) | copy-start | bytes 3076
  0.6 4.5 %copy-start.7 = (s32[16,16]{1,0:T(8,128)S(1)}, s32[16,16]{1,0:T(8,128)}, u32[]{:S(2)}) copy-start(s32[16,16]{1,0:T(8,128)} %tgt.3) | copy-start | bytes 3076
  0.7 4.5 %copy-start.6 = (s32[16,16]{1,0:T(8,128)S(1)}, s32[16,16]{1,0:T(8,128)}, u32[]{:S(2)}) copy-start(s32[16,16]{1,0:T(8,128)} %src.3) | copy-start | bytes 3076
  0.7 4.5 %copy-start.4 = (bf16[16,64,128]{2,1,0:T(8,128)(2,1)S(1)}, bf16[16,64,128]{2,1,0:T(8,128)(2,1)}, u32[]{:S(2)}) copy-start(bf16[16,64,128]{2,1,0:T(8,128)(2,1)} %load.3) | copy-start | bytes 786436
  0.7 4.5 %copy-start.3 = (bf16[16,64,128]{2,1,0:T(8,128)(2,1)S(1)}, bf16[16,64,128]{2,1,0:T(8,128)(2,1)}, u32[]{:S(2)}) copy-start(bf16[16,64,128]{2,1,0:T(8,128)(2,1)} %dev.3) | copy-start | bytes 786436
  0.7 4.5 %copy-start.1 = (bf16[16,128,512]{2,1,0:T(8,128)(2,1)S(1)}, bf16[16,128,512]{2,1,0:T(8,128)(2,1)}, u32[]{:S(2)}) copy-start(bf16[16,128,512]{2,1,0:T(8,128)(2,1)} %cond.3) | copy-start | bytes 6291460
  0.7 4.5 %copy-start.2 = (bf16[16,128,128]{2,1,0:T(8,128)(2,1)S(1)}, bf16[16,128,128]{2,1,0:T(8,128)(2,1)}, u32[]{:S(2)}) copy-start(bf16[16,128,128]{2,1,0:T(8,128)(2,1)} %jac.1) | copy-start | bytes 1572868
  1.7 4.9 %collective-permute-start = (bf16[80,128]{1,0:T(8,128)(2,1)S(1)}, bf16[80,128]{1,0:T(8,128)(2,1)S(1)}, u32[]{:S(2)}, u32[]{:S(2)}) collective-permute-start(bf16[80,128]{1,0:T(8,128)(2,1)S(1)} %get-tuple-element.13), channel_id=1, source_target_pairs={{0,28},{4,8},{8,4},{12,16},{16,12},{20,24},{24,20},{28,0},{1,29},{... | collective-permute-start | bytes 61448 | tf_op jit(solution)/shard_map/ppermute | solution.py:262
  5.1 10.7 %copy-start = (bf16[1,8,512,512]{3,2,1,0:T(8,128)(2,1)S(1)}, bf16[1,8,512,512]{3,2,1,0:T(8,128)(2,1)}, u32[]{:S(2)}) copy-start(bf16[1,8,512,512]{3,2,1,0:T(8,128)(2,1)} %param.16) | copy-start | bytes 12582916
  5.1 10.7 %copy-start.5 = (f32[1,8,512]{2,1,0:T(8,128)S(1)}, f32[1,8,512]{2,1,0:T(8,128)}, u32[]{:S(2)}) copy-start(f32[1,8,512]{2,1,0:T(8,128)} %param.17) | copy-start | bytes 49156
  5.1 1.5 %collective-permute-start.1 = (bf16[80,128]{1,0:T(8,128)(2,1)S(1)}, bf16[80,128]{1,0:T(8,128)(2,1)S(1)}, u32[]{:S(2)}, u32[]{:S(2)}) collective-permute-start(bf16[80,128]{1,0:T(8,128)(2,1)S(1)} %get-tuple-element.14), channel_id=1, source_target_pairs={{0,4},{4,0},{8,12},{12,8},{16,20},{20,16},{24,28},{28,24},{1,5},{5... | collective-permute-start | bytes 61448 | tf_op jit(solution)/shard_map/ppermute | solution.py:263

commit v4 on v3

--- a/solution.py
+++ b/solution.py
@@ -33,6 +33,14 @@
     upper = flow.astype(BF16).astype(F32)
     lane = lax.broadcasted_iota(I32, flow.shape, 1)
     return jnp.where(lane % (2 * edges) < edges, upper, flow - upper).astype(BF16)
+
+
+def folded(row):
+    return jnp.concatenate([row[:, 128 * k : 128 * k + 128] for k in range(row.shape[1] // 128)], axis=0)
+
+
+def unfolded(rows):
+    return jnp.concatenate([rows[k : k + 1] for k in range(rows.shape[0])], axis=1)
 
 
 def row_chunks(total, size, body):
@@ -131,7 +139,7 @@
     row_chunks(total, 64, body)
 
 
-def ends_kernel(dev, load, src, tgt, adm, cond, chip_in, pair_in, ends, part, mis, out):
+def ends_kernel(dev, load, src, tgt, adm, cond, chip_in, pair_in, ends, part, keep, mis, out):
     blocks, total, width = dev.shape
     edges = src.shape[1]
     last = blocks - 1
@@ -150,6 +158,17 @@
     tgt_last = hot_columns(twice(tgt[last : last + 1]), width)
     adm_last = jnp.where(place == count - 1, 0.0, twice(adm[last : last + 1]))
     right = jnp.concatenate([cond[0], cond[last]], axis=0)
+    reach = cond.shape[2]
+    rate = keep[...]
+    while rate.shape[0] > 1:
+        half = rate.shape[0] // 2
+        rate = rate[0:half] * rate[half : 2 * half]
+    rate = folded(rate)
+    upper = rate.astype(BF16).astype(F32)
+    rate = jnp.concatenate([upper, rate - upper], axis=0)
+    size = rate.shape[0]
+    for k in range(0, total, 2 * size):
+        out[k : k + 2 * size, reach : reach + 128] = jnp.concatenate([rate, rate], axis=0).astype(BF16)
 
     def body(here):
         pair_rows, chip_rows = pair_in[here, :].astype(F32), chip_in[here, :].astype(F32)
@@ -163,12 +182,12 @@
         mis[0, here, :] = low
         mis[1, here, :] = high
         sums = part[here, :] + dot(jnp.concatenate([low, high], axis=1), right)
-        out[here, :] = sums.astype(BF16)
+        out[here, 0:reach] = sums.astype(BF16)
 
     row_chunks(total, 64, body)
 
 
-def push_kernel(parts, gain, keep, inner, outer, states, running, sent, mis, sems):
+def push_kernel(parts, gain, keep, inner, outer, states, running, rates, sent, mis, sems):
     last = inner.shape[0] - 1
     copies_out = [
         pltpu.make_async_copy(inner.at[pl.ds(1, last - 1)], mis.at[pl.ds(1, last - 1)], sems.at[0]),
@@ -177,11 +196,13 @@
     ]
     for copy in copies_out:
         copy.start()
-    count, rows, width = parts.shape
-    copies = sent.shape[0]
+    count, rows, _ = parts.shape
+    width = gain.shape[2]
+    tiles = width // 128
+    place, group = lax.axis_index("bus"), lax.axis_index("period")
 
     def add(k, total):
-        return total + parts[k].astype(F32)
+        return total + parts[k, :, 0:width].astype(F32)
 
     section_in = lax.fori_loop(0, count, add, jnp.zeros((rows, width), F32), unroll=8).astype(BF16)
     line = lax.broadcasted_iota(I32, (rows, width), 0)
@@ -197,26 +218,49 @@
         shift *= 2
     states[...] = state
     running[...] = rate
-    tiles = width // 128
-    lines = [rate[rows - 1 : rows, 128 * k : 128 * k + 128] for k in range(tiles)]
-    lines += [state[rows - 1 : rows, 128 * k : 128 * k + 128] for k in range(tiles)]
-    both = jnp.concatenate(lines, axis=0)
-    for k in range(copies):
-        sent[k] = both
+
+    def gather(k, carried):
+        after, whole = carried
+        both = parts[k, :, width : width + 128].astype(F32)
+        span = both[0:tiles] + both[tiles : 2 * tiles]
+        rates[k] = span
+        return (after * jnp.where(k > place, span, 1.0), whole * span)
+
+    ones = jnp.ones((tiles, 128), F32)
+    after, whole = lax.fori_loop(0, count, gather, (ones, ones), unroll=8)
+    upper = whole.astype(BF16).astype(F32)
+    share = jnp.where(place % 2 == 0, upper, whole - upper)
+    last_state = folded(state[rows - 1 : rows])
+    here = jnp.concatenate([last_state, share], axis=0)
+    beyond = jnp.concatenate([last_state * after, share], axis=0)
+    for q in range(sent.shape[0] // count):
+        value = jnp.where(group == q, here, beyond).astype(BF16)
+        for k in range(count):
+            sent[q * count + k] = value
     for copy in copies_out:
         copy.wait()
 
 
-def enter_kernel(spans, states, running, out):
-    tiles = spans.shape[1] // 2
-    place = lax.axis_index("period") * lax.axis_size("bus") + lax.axis_index("bus")
+def enter_kernel(spans, rates, states, running, out):
+    count, tiles, _ = rates.shape
+    place, group = lax.axis_index("bus"), lax.axis_index("period")
+
+    def add(k, total):
+        return total + spans[k].astype(F32)
+
+    entering = jnp.zeros((tiles, 128), F32)
+    for q in range(spans.shape[0] // count - 1):
+        first = q * count
+        total = lax.fori_loop(first, first + count, add, jnp.zeros((2 * tiles, 128), F32), unroll=8)[0:tiles]
+        pair = (spans[first].astype(F32) + spans[first + 1].astype(F32))[tiles : 2 * tiles]
+        entering = jnp.where(q < group, pair * entering + total, entering)
 
     def step(k, entering):
-        return spans[k, 0:tiles] * entering + spans[k, tiles : 2 * tiles]
-
-    entering = lax.fori_loop(0, place, step, jnp.zeros((tiles, 128), F32))
-    flat = jnp.concatenate([entering[k : k + 1] for k in range(tiles)], axis=1)
-    out[...] = states[...] + running[...] * flat
+        state = spans[group * count + k].astype(F32)[0:tiles]
+        return jnp.where(k < place, rates[k] * entering + state, entering)
+
+    entering = lax.fori_loop(0, count, step, entering, unroll=8)
+    out[...] = states[...] + running[...] * unfolded(entering)
 
 
 def call(kernel, shapes, inputs, cost, scratch=(), specs=None, ins=None):
@@ -258,8 +302,16 @@
         ins=[HBM] * 5,
     )
     pairs = [(k, k ^ 1) for k in range(count)]
-    chips = [(k, (k + 1) % count if k % 2 else (k - 1) % count) for k in range(count)]
-    chip_in = lax.ppermute(chip_out, "bus", chips)
+    groups = lax.axis_size("period")
+    chips = []
+    for k in range(count):
+        partner = k + 1 if k % 2 else k - 1
+        for g in range(groups):
+            if 0 <= partner < count:
+                chips.append((k * groups + g, partner * groups + g))
+            else:
+                chips.append((k * groups + g, k * groups + g ^ 1))
+    chip_in = lax.ppermute(chip_out, ("bus", "period"), chips)
     pair_in = lax.ppermute(pair_out, "bus", pairs)
     inner, ends, part = call(
         inner_kernel,
@@ -269,27 +321,28 @@
     )
     outer, sums = call(
         ends_kernel,
-        [shape((2, total, width), BF16), shape((total, states_width), BF16)],
-        (deviation, loading, tie_source, tie_target, tie_admittance, condense, chip_in, pair_in, ends, part),
+        [shape((2, total, width), BF16), shape((total, states_width + 128), BF16)],
+        (deviation, loading, tie_source, tie_target, tie_admittance, condense, chip_in, pair_in, ends, part, retention[0]),
         1.0,
     )
-    parts = lax.all_to_all(sums.reshape(count, rows, states_width), "bus", 0, 0, tiled=True)
+    parts = lax.all_to_all(sums.reshape(count, rows, states_width + 128), "bus", 0, 0, tiled=True)
     tiles = 2 * states_width // 128
-    states, running, sent, mismatch = call(
+    states, running, rates, sent, mismatch = call(
         push_kernel,
         [
             shape((rows, states_width), F32),
             shape((rows, states_width), F32),
-            shape((spans, tiles, 128), F32),
+            shape((count, tiles // 2, 128), F32),
+            shape((spans, tiles, 128), BF16),
             shape((blocks, total, width), BF16),
         ],
         (parts, section_gain[0], retention[0], inner, outer),
         2.0,
         [pltpu.SemaphoreType.DMA((3,))],
-        [VM, VM, VM, HBM],
+        [VM, VM, VM, VM, HBM],
     )
     everything = lax.all_to_all(sent, ("period", "bus"), 0, 0, tiled=True)
-    out = call(enter_kernel, shape((rows, states_width), F32), (everything, states, running), 1.0)
+    out = call(enter_kernel, shape((rows, states_width), F32), (everything, rates, states, running), 1.0)
     return (mismatch, out[None])
 
 

time: 29.9 us -> 29.1 us (0.973)
  blocking collectives: 20.7 us -> 19.9 us
    all_to_all x1, blocking collectives: 12 us -> 11.2 us  [shards(): everything = lax.all_to_all(sent, ('period', 'bus'), 0, 0, tiled=True)]
    ppermute x1, starting transfers between devices: 3.4 us -> 3.09 us  [shards(): chip_in = lax.ppermute(chip_out, ('bus', 'period'), chips)]
  transfers between devices with their start and end apart: 2 -> 2, of which waited for: 1 -> 1; matrix products, arithmetic and copies ran while one was open for 0% -> 0% of each run, Pallas kernels for 4% -> 5%
where the time goes in v4:
time: 29.1 us; the launch traced here: 28.9 us
  blocking collectives  19.9 us (68%)
  Pallas kernels  4.73 us (16%)
  starting transfers between devices  3.12 us (11%)
  between operations  0.75 us (3%)
  waiting for transfers between devices  0.38 us (1%)
    all_to_all x1, blocking collectives, shards(): everything = lax.all_to_all(sent, ('period', 'bus'), 0, 0, tiled=True)  11.2 us
    all_to_all x1, blocking collectives, shards(): lax.all_to_all(sums.reshape(count, rows, states_width + 128), 'bus', 0, 0...  8.67 us
    pallas_call x5, Pallas kernels, call(): pl.pallas_call(kernel, out_shape=shapes, in_specs=ins or [VM] * len(input...  4.73 us
    ppermute x1, starting transfers between devices, shards(): chip_in = lax.ppermute(chip_out, ('bus', 'period'), chips)  3.09 us
  transfers between devices with their start and end apart: 2, of which 1 were waited for; matrix products, arithmetic and copies ran while one was open for 0% of the time, Pallas kernels for 5%

profile of v4, /device:TPU:0, one launch (start us, length us, event | category | flops | bytes accessed | tf_op | source)
XLA Modules:
  0.0 28.9 jit_solution(13771721987916439306)
XLA Ops:
  0.6 0.0 copy-start.8
  0.6 0.0 copy-start.7
  0.7 0.0 copy-start.6
  0.7 0.0 copy-start.4
  0.7 0.0 copy-start.3
  0.7 0.0 copy-start.1
  0.7 0.0 copy-start.2
  0.7 1.0 %shard_map.104 = (bf16[80,128]{1,0:T(8,128)(2,1)S(1)}, bf16[80,128]{1,0:T(8,128)(2,1)S(1)}) custom-call(bf16[16,64,128]{2,1,0:T(8,128)(2,1)} %dev.3, bf16[16,64,128]{2,1,0:T(8,128)(2,1)} %load.3, s32[16,16]{1,0:T(8,128)} %src.3, s32[16,16]{1,0:T(8,128)} %tgt.3, f32[16,16]{1,0:T(8,128)} %adm.3), custom_call_target="tpu_custom_call" | custom-call | flops 10000000000 | bytes 30000000 | tf_op jit(solution)/shard_map/pallas_call | solution.py:268
  1.7 3.1 %collective-permute-start = (bf16[80,128]{1,0:T(8,128)(2,1)S(1)}, bf16[80,128]{1,0:T(8,128)(2,1)S(1)}, u32[]{:S(2)}, u32[]{:S(2)}) collective-permute-start(bf16[80,128]{1,0:T(8,128)(2,1)S(1)} %get-tuple-element.14), channel_id=1, source_target_pairs={{0,1},{1,0},{2,3},{3,2},{4,8},{5,9},{6,10},{7,11},{8,4},{9,5},{10,... | collective-permute-start | bytes 61448 | tf_op jit(solution)/shard_map/ppermute | solution.py:314
  4.8 0.0 copy-start.5
  4.8 0.0 copy-start
  4.8 0.0 collective-permute-start.1
  4.8 0.0 copy-done.8
  4.8 0.0 copy-done.7
  4.8 0.0 copy-done.6
  4.8 0.0 copy-done.4
  4.8 0.0 copy-done.3
  4.9 0.0 copy-done.1
  4.9 0.0 copy-done.2
  4.9 1.3 %shard_map.105 = (bf16[16,64,128]{2,1,0:T(8,128)(2,1)S(1)}, f32[2,64,128]{2,1,0:T(8,128)S(1)}, f32[64,512]{1,0:T(8,128)S(1)}) custom-call(bf16[16,64,128]{2,1,0:T(8,128)(2,1)S(1)} %copy-done.3, bf16[16,64,128]{2,1,0:T(8,128)(2,1)S(1)} %copy-done.4, bf16[16,128,128]{2,1,0:T(8,128)(2,1)S(1)} %copy-done.2, s32[16,16]{1,0:T(8,128)S(1)} %copy-done.6, ...), custom_call_target="tpu_custom_call" | custom-call | flops 5000000000 | bytes 15000000 | tf_op jit(solution)/shard_map/pallas_call | solution.py:268
  6.2 0.4 %collective-permute-done.chip_in = bf16[80,128]{1,0:T(8,128)(2,1)S(1)} collective-permute-done((bf16[80,128]{1,0:T(8,128)(2,1)S(1)}, bf16[80,128]{1,0:T(8,128)(2,1)S(1)}, u32[]{:S(2)}, u32[]{:S(2)}) %collective-permute-start) | collective-permute-done | bytes 20512 | tf_op jit(solution)/shard_map/ppermute | solution.py:314
  6.6 0.0 collective-permute-done.1.pair_in
  6.6 0.0 copy-done.5
  6.6 0.5 %shard_map.106 = (bf16[2,64,128]{2,1,0:T(8,128)(2,1)S(1)}, bf16[64,640]{1,0:T(8,128)(2,1)S(1)}) custom-call(bf16[16,64,128]{2,1,0:T(8,128)(2,1)S(1)} %copy-done.3, bf16[16,64,128]{2,1,0:T(8,128)(2,1)S(1)} %copy-done.4, s32[16,16]{1,0:T(8,128)S(1)} %copy-done.6, s32[16,16]{1,0:T(8,128)S(1)} %copy-done.7, f32[16,16]{1,0:T(8,128)S(1)} %copy-done.8, ...), custom_call_target="tpu_custom_call" | custom-call | flops 1000000000 | bytes 3000000 | tf_op jit(solution)/shard_map/pallas_call | solution.py:268
  7.0 8.7 %all_to_all.10.parts = bf16[8,8,640]{2,1,0:T(8,128)(2,1)S(1)} all-to-all(bf16[8,8,640]{2,1,0:T(8,128)(2,1)S(1)} %bitcast.4), channel_id=1, replica_groups=mesh['bus'=8,'period'=4] {'bus'}, dimensions={0} | all-to-all | bytes 163840 | tf_op jit(solution)/shard_map/all_to_all | solution.py:328
  15.7 0.0 copy-done
  15.7 1.3 %shard_map.107 = (f32[8,512]{1,0:T(8,128)S(1)}, f32[8,512]{1,0:T(8,128)S(1)}, f32[8,4,128]{2,1,0:T(4,128)S(1)}, bf16[32,8,128]{2,1,0:T(8,128)(2,1)S(1)}, bf16[16,64,128]{2,1,0:T(8,128)(2,1)}) custom-call(bf16[8,8,640]{2,1,0:T(8,128)(2,1)S(1)} %all_to_all.10.parts, bf16[8,512,512]{2,1,0:T(8,128)(2,1)S(1)} %bitcast.5, f32[8,512]{1,0:T(8,128)S(1)} %bitcast.7, ...), custom_call_target="tpu_custom_call" | custom-call | flops 2000000000 | bytes 6000000 | tf_op jit(solution)/shard_map/pallas_call | solution.py:268
  17.0 11.2 %all_to_all.11.spans = bf16[32,8,128]{2,1,0:T(8,128)(2,1)S(1)} all-to-all(bf16[32,8,128]{2,1,0:T(8,128)(2,1)S(1)} %get-tuple-element.22), channel_id=1, replica_groups=mesh['bus'=8,'period'=4] {'period','bus'}, dimensions={0} | all-to-all | bytes 131072 | tf_op jit(solution)/shard_map/all_to_all | solution.py:344
  28.2 0.6 %shard_map.108 = f32[8,512]{1,0:T(8,128)} custom-call(bf16[32,8,128]{2,1,0:T(8,128)(2,1)S(1)} %all_to_all.11.spans, f32[8,4,128]{2,1,0:T(4,128)S(1)} %get-tuple-element.23.rates, f32[8,512]{1,0:T(8,128)S(1)} %get-tuple-element.24.states, f32[8,512]{1,0:T(8,128)S(1)} %get-tuple-element.25.running), custom_call_target="tpu_custom_call" | custom-call | flops 1000000000 | bytes 3000000 | tf_op jit(solution)/shard_map/pallas_call | solution.py:268
Async XLA Ops:
  0.6 4.2 %copy-start.8 = (f32[16,16]{1,0:T(8,128)S(1)}, f32[16,16]{1,0:T(8,128)}, u32[]{:S(2)}) copy-start(f32[16,16]{1,0:T(8,128)} %adm.3) | copy-start | bytes 3076
  0.6 4.2 %copy-start.7 = (s32[16,16]{1,0:T(8,128)S(1)}, s32[16,16]{1,0:T(8,128)}, u32[]{:S(2)}) copy-start(s32[16,16]{1,0:T(8,128)} %tgt.3) | copy-start | bytes 3076
  0.7 4.2 %copy-start.6 = (s32[16,16]{1,0:T(8,128)S(1)}, s32[16,16]{1,0:T(8,128)}, u32[]{:S(2)}) copy-start(s32[16,16]{1,0:T(8,128)} %src.3) | copy-start | bytes 3076
  0.7 4.2 %copy-start.4 = (bf16[16,64,128]{2,1,0:T(8,128)(2,1)S(1)}, bf16[16,64,128]{2,1,0:T(8,128)(2,1)}, u32[]{:S(2)}) copy-start(bf16[16,64,128]{2,1,0:T(8,128)(2,1)} %load.3) | copy-start | bytes 786436
  0.7 4.2 %copy-start.3 = (bf16[16,64,128]{2,1,0:T(8,128)(2,1)S(1)}, bf16[16,64,128]{2,1,0:T(8,128)(2,1)}, u32[]{:S(2)}) copy-start(bf16[16,64,128]{2,1,0:T(8,128)(2,1)} %dev.3) | copy-start | bytes 786436
  0.7 4.2 %copy-start.1 = (bf16[16,128,512]{2,1,0:T(8,128)(2,1)S(1)}, bf16[16,128,512]{2,1,0:T(8,128)(2,1)}, u32[]{:S(2)}) copy-start(bf16[16,128,512]{2,1,0:T(8,128)(2,1)} %cond.3) | copy-start | bytes 6291460
  0.7 4.2 %copy-start.2 = (bf16[16,128,128]{2,1,0:T(8,128)(2,1)S(1)}, bf16[16,128,128]{2,1,0:T(8,128)(2,1)}, u32[]{:S(2)}) copy-start(bf16[16,128,128]{2,1,0:T(8,128)(2,1)} %jac.1) | copy-start | bytes 1572868
  1.7 4.9 %collective-permute-start = (bf16[80,128]{1,0:T(8,128)(2,1)S(1)}, bf16[80,128]{1,0:T(8,128)(2,1)S(1)}, u32[]{:S(2)}, u32[]{:S(2)}) collective-permute-start(bf16[80,128]{1,0:T(8,128)(2,1)S(1)} %get-tuple-element.14), channel_id=1, source_target_pairs={{0,1},{1,0},{2,3},{3,2},{4,8},{5,9},{6,10},{7,11},{8,4},{9,5},{10,... | collective-permute-start | bytes 61448 | tf_op jit(solution)/shard_map/ppermute | solution.py:314
  4.8 1.8 %copy-start.5 = (f32[1,8,512]{2,1,0:T(8,128)S(1)}, f32[1,8,512]{2,1,0:T(8,128)}, u32[]{:S(2)}) copy-start(f32[1,8,512]{2,1,0:T(8,128)} %param.17) | copy-start | bytes 49156
  4.8 10.9 %copy-start = (bf16[1,8,512,512]{3,2,1,0:T(8,128)(2,1)S(1)}, bf16[1,8,512,512]{3,2,1,0:T(8,128)(2,1)}, u32[]{:S(2)}) copy-start(bf16[1,8,512,512]{3,2,1,0:T(8,128)(2,1)} %param.16) | copy-start | bytes 12582916
  4.8 1.8 %collective-permute-start.1 = (bf16[80,128]{1,0:T(8,128)(2,1)S(1)}, bf16[80,128]{1,0:T(8,128)(2,1)S(1)}, u32[]{:S(2)}, u32[]{:S(2)}) collective-permute-start(bf16[80,128]{1,0:T(8,128)(2,1)S(1)} %get-tuple-element.15), channel_id=1, source_target_pairs={{0,4},{4,0},{8,12},{12,8},{16,20},{20,16},{24,28},{28,24},{1,5},{5... | collective-permute-start | bytes 61448 | tf_op jit(solution)/shard_map/ppermute | solution.py:315

commit v5 on v4

--- a/solution.py
+++ b/solution.py
@@ -94,7 +94,7 @@
     chip_out[rows : rows + TIE_ROWS, :] = packed
 
 
-def inner_kernel(dev, load, jac, src, tgt, adm, cond, mis, ends, part):
+def inner_kernel(dev, load, jac, src, tgt, adm, cond, mis_hbm, ends, part, mis, sem):
     blocks, total, width = dev.shape
     edges = src.shape[1]
     src4 = jnp.concatenate([src[...]] * 4, axis=1)
@@ -127,6 +127,9 @@
                 rounded = whole.astype(BF16)
                 mis[b, here, :] = rounded
                 row.append((b, rounded))
+        middle = pl.ds(1, blocks - 2)
+        copy = pltpu.make_async_copy(mis.at[middle, here, :], mis_hbm.at[middle, here, :], sem)
+        copy.start()
         sums = 0.0
         for k in range(0, len(row), 2):
             pair = row[k : k + 2]
@@ -135,6 +138,7 @@
             right = cond[first : first + len(pair)].reshape(len(pair) * width, cond.shape[2])
             sums = sums + dot(left, right)
         part[here, :] = sums
+        copy.wait()
 
     row_chunks(total, 64, body)
 
@@ -187,15 +191,7 @@
     row_chunks(total, 64, body)
 
 
-def push_kernel(parts, gain, keep, inner, outer, states, running, rates, sent, mis, sems):
-    last = inner.shape[0] - 1
-    copies_out = [
-        pltpu.make_async_copy(inner.at[pl.ds(1, last - 1)], mis.at[pl.ds(1, last - 1)], sems.at[0]),
-        pltpu.make_async_copy(outer.at[0], mis.at[0], sems.at[1]),
-        pltpu.make_async_copy(outer.at[1], mis.at[last], sems.at[2]),
-    ]
-    for copy in copies_out:
-        copy.start()
+def push_kernel(parts, gain, keep, states, running, rates, sent):
     count, rows, _ = parts.shape
     width = gain.shape[2]
     tiles = width // 128
@@ -237,11 +233,13 @@
         value = jnp.where(group == q, here, beyond).astype(BF16)
         for k in range(count):
             sent[q * count + k] = value
-    for copy in copies_out:
-        copy.wait()
-
-
-def enter_kernel(spans, rates, states, running, out):
+
+
+def enter_kernel(spans, rates, states, running, outer, mis_in, out_hbm, mis, out, sems):
+    blocks = mis.shape[0]
+    copies = [pltpu.make_async_copy(outer.at[k], mis.at[k * (blocks - 1)], sems.at[k]) for k in range(2)]
+    for copy in copies:
+        copy.start()
     count, tiles, _ = rates.shape
     place, group = lax.axis_index("bus"), lax.axis_index("period")
 
@@ -261,9 +259,13 @@
 
     entering = lax.fori_loop(0, count, step, entering, unroll=8)
     out[...] = states[...] + running[...] * unfolded(entering)
-
-
-def call(kernel, shapes, inputs, cost, scratch=(), specs=None, ins=None):
+    copies.append(pltpu.make_async_copy(out, out_hbm, sems.at[2]))
+    copies[2].start()
+    for copy in copies:
+        copy.wait()
+
+
+def call(kernel, shapes, inputs, cost, scratch=(), specs=None, ins=None, aliases=None):
     single = not isinstance(shapes, (list, tuple))
     return pl.pallas_call(
         kernel,
@@ -271,6 +273,7 @@
         in_specs=ins or [VM] * len(inputs),
         out_specs=specs or (VM if single else [VM] * len(shapes)),
         scratch_shapes=list(scratch),
+        input_output_aliases=aliases or {},
         compiler_params=PARAMS,
         cost_estimate=pl.CostEstimate(flops=int(cost * 1e9), transcendentals=0, bytes_accessed=int(cost * 3.0e6)),
     )(*inputs)
@@ -318,6 +321,8 @@
         [shape((blocks, total, width), BF16), shape((2, total, width), F32), shape((total, states_width), F32)],
         (deviation, loading, jacobian, tie_source, tie_target, tie_admittance, condense),
         5.0,
+        [pltpu.VMEM((blocks, total, width), BF16), pltpu.SemaphoreType.DMA],
+        [HBM, VM, VM],
     )
     outer, sums = call(
         ends_kernel,
@@ -327,22 +332,28 @@
     )
     parts = lax.all_to_all(sums.reshape(count, rows, states_width + 128), "bus", 0, 0, tiled=True)
     tiles = 2 * states_width // 128
-    states, running, rates, sent, mismatch = call(
+    states, running, rates, sent = call(
         push_kernel,
         [
             shape((rows, states_width), F32),
             shape((rows, states_width), F32),
             shape((count, tiles // 2, 128), F32),
             shape((spans, tiles, 128), BF16),
-            shape((blocks, total, width), BF16),
         ],
-        (parts, section_gain[0], retention[0], inner, outer),
+        (parts, section_gain[0], retention[0]),
         2.0,
-        [pltpu.SemaphoreType.DMA((3,))],
-        [VM, VM, VM, VM, HBM],
     )
     everything = lax.all_to_all(sent, ("period", "bus"), 0, 0, tiled=True)
-    out = call(enter_kernel, shape((rows, states_width), F32), (everything, rates, states, running), 1.0)
+    out, mismatch = call(
+        enter_kernel,
+        [shape((rows, states_width), F32), shape((blocks, total, width), BF16)],
+        (everything, rates, states, running, outer, inner),
+        1.0,
+        [pltpu.VMEM((rows, states_width), F32), pltpu.SemaphoreType.DMA((3,))],
+        [HBM, HBM],
+        [VM] * 5 + [HBM],
+        {5: 1},
+    )
     return (mismatch, out[None])
 
 

time: 29.1 us -> 28.5 us (0.979)
  waiting for transfers between devices: 0.38 us -> 0.01 us
    ppermute x1, waiting for transfers between devices: 0.38 us -> 0.01 us  [shards(): chip_in = lax.ppermute(chip_out, ('bus', 'period'), chips)]
  transfers between devices with their start and end apart: 2 -> 2, of which waited for: 1 -> 0; matrix products, arithmetic and copies ran while one was open for 0% -> 0% of each run, Pallas kernels for 5% -> 6%
where the time goes in v5:
time: 28.5 us; the launch traced here: 28.3 us
  blocking collectives  19.8 us (69%)
  Pallas kernels  4.53 us (16%)
  starting transfers between devices  3.12 us (11%)
  between operations  0.77 us (3%)
    all_to_all x1, blocking collectives, shards(): everything = lax.all_to_all(sent, ('period', 'bus'), 0, 0, tiled=True)  11.2 us
    all_to_all x1, blocking collectives, shards(): lax.all_to_all(sums.reshape(count, rows, states_width + 128), 'bus', 0, 0...  8.61 us
    pallas_call x5, Pallas kernels, call(): pl.pallas_call(kernel, out_shape=shapes, in_specs=ins or [VM] * len(input...  4.53 us
    ppermute x1, starting transfers between devices, shards(): chip_in = lax.ppermute(chip_out, ('bus', 'period'), chips)  3.09 us
  transfers between devices with their start and end apart: 2, of which 0 were waited for; matrix products, arithmetic and copies ran while one was open for 0% of the time, Pallas kernels for 6%

profile of v5, /device:TPU:0, one launch (start us, length us, event | category | flops | bytes accessed | tf_op | source)
XLA Modules:
  0.0 28.3 jit_solution(11032697207394763064)
XLA Ops:
  0.6 0.0 copy-start.8
  0.6 0.0 copy-start.7
  0.7 0.0 copy-start.6
  0.7 0.0 copy-start.4
  0.7 0.0 copy-start.3
  0.7 0.0 copy-start.1
  0.7 0.0 copy-start.2
  0.7 1.0 %shard_map.104 = (bf16[80,128]{1,0:T(8,128)(2,1)S(1)}, bf16[80,128]{1,0:T(8,128)(2,1)S(1)}) custom-call(bf16[16,64,128]{2,1,0:T(8,128)(2,1)} %dev.3, bf16[16,64,128]{2,1,0:T(8,128)(2,1)} %load.3, s32[16,16]{1,0:T(8,128)} %src.3, s32[16,16]{1,0:T(8,128)} %tgt.3, f32[16,16]{1,0:T(8,128)} %adm.3), custom_call_target="tpu_custom_call" | custom-call | flops 10000000000 | bytes 30000000 | tf_op jit(solution)/shard_map/pallas_call | solution.py:270
  1.7 3.1 %collective-permute-start = (bf16[80,128]{1,0:T(8,128)(2,1)S(1)}, bf16[80,128]{1,0:T(8,128)(2,1)S(1)}, u32[]{:S(2)}, u32[]{:S(2)}) collective-permute-start(bf16[80,128]{1,0:T(8,128)(2,1)S(1)} %get-tuple-element.15), channel_id=1, source_target_pairs={{0,1},{1,0},{2,3},{3,2},{4,8},{5,9},{6,10},{7,11},{8,4},{9,5},{10,... | collective-permute-start | bytes 61448 | tf_op jit(solution)/shard_map/ppermute | solution.py:317
  4.8 0.0 copy-start.5
  4.8 0.0 copy-start
  4.8 0.0 collective-permute-start.1
  4.8 0.0 copy-done.8
  4.8 0.0 copy-done.7
  4.8 0.0 copy-done.6
  4.8 0.0 copy-done.4
  4.8 0.0 copy-done.3
  4.9 0.0 copy-done.1
  4.9 0.0 copy-done.2
  4.9 1.7 %shard_map.105 = (bf16[16,64,128]{2,1,0:T(8,128)(2,1)}, f32[2,64,128]{2,1,0:T(8,128)S(1)}, f32[64,512]{1,0:T(8,128)S(1)}) custom-call(bf16[16,64,128]{2,1,0:T(8,128)(2,1)S(1)} %copy-done.3, bf16[16,64,128]{2,1,0:T(8,128)(2,1)S(1)} %copy-done.4, bf16[16,128,128]{2,1,0:T(8,128)(2,1)S(1)} %copy-done.2, s32[16,16]{1,0:T(8,128)S(1)} %copy-done.6, ...), custom_call_target="tpu_custom_call" | custom-call | flops 5000000000 | bytes 15000000 | tf_op jit(solution)/shard_map/pallas_call | solution.py:270
  6.6 0.0 collective-permute-done.chip_in
  6.6 0.0 collective-permute-done.1.pair_in
  6.6 0.0 copy-done.5
  6.6 0.5 %shard_map.106 = (bf16[2,64,128]{2,1,0:T(8,128)(2,1)S(1)}, bf16[64,640]{1,0:T(8,128)(2,1)S(1)}) custom-call(bf16[16,64,128]{2,1,0:T(8,128)(2,1)S(1)} %copy-done.3, bf16[16,64,128]{2,1,0:T(8,128)(2,1)S(1)} %copy-done.4, s32[16,16]{1,0:T(8,128)S(1)} %copy-done.6, s32[16,16]{1,0:T(8,128)S(1)} %copy-done.7, f32[16,16]{1,0:T(8,128)S(1)} %copy-done.8, ...), custom_call_target="tpu_custom_call" | custom-call | flops 1000000000 | bytes 3000000 | tf_op jit(solution)/shard_map/pallas_call | solution.py:270
  7.1 8.6 %all_to_all.10.parts = bf16[8,8,640]{2,1,0:T(8,128)(2,1)S(1)} all-to-all(bf16[8,8,640]{2,1,0:T(8,128)(2,1)S(1)} %bitcast.4), channel_id=1, replica_groups=mesh['bus'=8,'period'=4] {'bus'}, dimensions={0} | all-to-all | bytes 163840 | tf_op jit(solution)/shard_map/all_to_all | solution.py:333
  15.7 0.0 copy-done
  15.7 0.7 %shard_map.107 = (f32[8,512]{1,0:T(8,128)S(1)}, f32[8,512]{1,0:T(8,128)S(1)}, f32[8,4,128]{2,1,0:T(4,128)S(1)}, bf16[32,8,128]{2,1,0:T(8,128)(2,1)S(1)}) custom-call(bf16[8,8,640]{2,1,0:T(8,128)(2,1)S(1)} %all_to_all.10.parts, bf16[8,512,512]{2,1,0:T(8,128)(2,1)S(1)} %bitcast.5, f32[8,512]{1,0:T(8,128)S(1)} %bitcast.7), custom_call_target="tpu_custom_call" | custom-call | flops 2000000000 | bytes 6000000 | tf_op jit(solution)/shard_map/pallas_call | solution.py:270
  16.4 11.2 %all_to_all.11.spans = bf16[32,8,128]{2,1,0:T(8,128)(2,1)S(1)} all-to-all(bf16[32,8,128]{2,1,0:T(8,128)(2,1)S(1)} %get-tuple-element.20), channel_id=1, replica_groups=mesh['bus'=8,'period'=4] {'period','bus'}, dimensions={0} | all-to-all | bytes 131072 | tf_op jit(solution)/shard_map/all_to_all | solution.py:346
  27.6 0.7 %shard_map.108 = (f32[8,512]{1,0:T(8,128)}, bf16[16,64,128]{2,1,0:T(8,128)(2,1)}) custom-call(bf16[32,8,128]{2,1,0:T(8,128)(2,1)S(1)} %all_to_all.11.spans, f32[8,4,128]{2,1,0:T(4,128)S(1)} %get-tuple-element.21.rates, f32[8,512]{1,0:T(8,128)S(1)} %get-tuple-element.22.states, ...), custom_call_target="tpu_custom_call", output_to_operand_aliasing={{1}: (5, {})} | custom-call | flops 1000000000 | bytes 3000000 | tf_op jit(solution)/shard_map/pallas_call | solution.py:270
Async XLA Ops:
  0.6 4.2 %copy-start.8 = (f32[16,16]{1,0:T(8,128)S(1)}, f32[16,16]{1,0:T(8,128)}, u32[]{:S(2)}) copy-start(f32[16,16]{1,0:T(8,128)} %adm.3) | copy-start | bytes 3076
  0.6 4.2 %copy-start.7 = (s32[16,16]{1,0:T(8,128)S(1)}, s32[16,16]{1,0:T(8,128)}, u32[]{:S(2)}) copy-start(s32[16,16]{1,0:T(8,128)} %tgt.3) | copy-start | bytes 3076
  0.7 4.2 %copy-start.6 = (s32[16,16]{1,0:T(8,128)S(1)}, s32[16,16]{1,0:T(8,128)}, u32[]{:S(2)}) copy-start(s32[16,16]{1,0:T(8,128)} %src.3) | copy-start | bytes 3076
  0.7 4.2 %copy-start.4 = (bf16[16,64,128]{2,1,0:T(8,128)(2,1)S(1)}, bf16[16,64,128]{2,1,0:T(8,128)(2,1)}, u32[]{:S(2)}) copy-start(bf16[16,64,128]{2,1,0:T(8,128)(2,1)} %load.3) | copy-start | bytes 786436
  0.7 4.2 %copy-start.3 = (bf16[16,64,128]{2,1,0:T(8,128)(2,1)S(1)}, bf16[16,64,128]{2,1,0:T(8,128)(2,1)}, u32[]{:S(2)}) copy-start(bf16[16,64,128]{2,1,0:T(8,128)(2,1)} %dev.3) | copy-start | bytes 786436
  0.7 4.2 %copy-start.1 = (bf16[16,128,512]{2,1,0:T(8,128)(2,1)S(1)}, bf16[16,128,512]{2,1,0:T(8,128)(2,1)}, u32[]{:S(2)}) copy-start(bf16[16,128,512]{2,1,0:T(8,128)(2,1)} %cond.3) | copy-start | bytes 6291460
  0.7 4.2 %copy-start.2 = (bf16[16,128,128]{2,1,0:T(8,128)(2,1)S(1)}, bf16[16,128,128]{2,1,0:T(8,128)(2,1)}, u32[]{:S(2)}) copy-start(bf16[16,128,128]{2,1,0:T(8,128)(2,1)} %jac.1) | copy-start | bytes 1572868
  1.7 4.9 %collective-permute-start = (bf16[80,128]{1,0:T(8,128)(2,1)S(1)}, bf16[80,128]{1,0:T(8,128)(2,1)S(1)}, u32[]{:S(2)}, u32[]{:S(2)}) collective-permute-start(bf16[80,128]{1,0:T(8,128)(2,1)S(1)} %get-tuple-element.15), channel_id=1, source_target_pairs={{0,1},{1,0},{2,3},{3,2},{4,8},{5,9},{6,10},{7,11},{8,4},{9,5},{10,... | collective-permute-start | bytes 61448 | tf_op jit(solution)/shard_map/ppermute | solution.py:317
  4.8 1.8 %copy-start.5 = (f32[1,8,512]{2,1,0:T(8,128)S(1)}, f32[1,8,512]{2,1,0:T(8,128)}, u32[]{:S(2)}) copy-start(f32[1,8,512]{2,1,0:T(8,128)} %param.17) | copy-start | bytes 49156
  4.8 10.9 %copy-start = (bf16[1,8,512,512]{3,2,1,0:T(8,128)(2,1)S(1)}, bf16[1,8,512,512]{3,2,1,0:T(8,128)(2,1)}, u32[]{:S(2)}) copy-start(bf16[1,8,512,512]{3,2,1,0:T(8,128)(2,1)} %param.16) | copy-start | bytes 12582916
  4.8 1.8 %collective-permute-start.1 = (bf16[80,128]{1,0:T(8,128)(2,1)S(1)}, bf16[80,128]{1,0:T(8,128)(2,1)S(1)}, u32[]{:S(2)}, u32[]{:S(2)}) collective-permute-start(bf16[80,128]{1,0:T(8,128)(2,1)S(1)} %get-tuple-element.16), channel_id=1, source_target_pairs={{0,4},{4,0},{8,12},{12,8},{16,20},{20,16},{24,28},{28,24},{1,5},{5... | collective-permute-start | bytes 61448 | tf_op jit(solution)/shard_map/ppermute | solution.py:318

commit v6 on v5

--- a/solution.py
+++ b/solution.py
@@ -8,6 +8,7 @@
 F32, BF16, I32 = jnp.float32, jnp.bfloat16, jnp.int32
 VM = pl.BlockSpec(memory_space=pltpu.VMEM)
 TIE_ROWS = 16
+SUMMED_ROWS = 2
 PARAMS = pltpu.CompilerParams(vmem_limit_bytes=16 * 1024 * 1024)
 HBM = pl.BlockSpec(memory_space=pltpu.HBM)
 
@@ -53,7 +54,7 @@
         body(pl.ds(pl.multiple_of(k * size, size), size))
 
 
-def halo_kernel(dev_hbm, load_hbm, src_hbm, tgt_hbm, adm_hbm, pair_out, chip_out, dev, load, src, tgt, adm, ties, sems):
+def halo_kernel(dev_hbm, load_hbm, src_hbm, tgt_hbm, adm_hbm, pair_out, chip_out, src, tgt, adm, dev, load, ties, sems):
     last = dev_hbm.shape[0] - 1
     rows = dev.shape[1]
     edges = src.shape[1]
@@ -94,6 +95,10 @@
     chip_out[rows : rows + TIE_ROWS, :] = packed
 
 
+def pass_kernel(given, same):
+    same[0:8, :] = given[0:8, :]
+
+
 def inner_kernel(dev, load, jac, src, tgt, adm, cond, mis_hbm, ends, part, mis, sem):
     blocks, total, width = dev.shape
     edges = src.shape[1]
@@ -202,9 +207,17 @@
 
     section_in = lax.fori_loop(0, count, add, jnp.zeros((rows, width), F32), unroll=8).astype(BF16)
     line = lax.broadcasted_iota(I32, (rows, width), 0)
+    columns = jnp.transpose(section_in.astype(F32))
     pushed = jnp.zeros((rows, width), F32)
     for r in range(rows):
-        pushed = jnp.where(line == r, dot(section_in, gain[r]), pushed)
+        if r < rows - SUMMED_ROWS:
+            row = dot(section_in, gain[r])
+        else:
+            row = jnp.zeros((16, width), F32)
+            for m in range(0, width, 16):
+                row = row + gain[r, m : m + 16, :].astype(F32) * columns[m : m + 16, r : r + 1]
+            row = jnp.sum(row, axis=0, keepdims=True)
+        pushed = jnp.where(line == r, row, pushed)
     rate, state = keep[...], pushed
     shift = 1
     while shift < rows:
@@ -288,22 +301,21 @@
     shape = jax.ShapeDtypeStruct
 
     payload = shape((total + TIE_ROWS, width), BF16)
-    pair_out, chip_out = call(
+    lines, weights = shape((blocks, edges), I32), shape((blocks, edges), F32)
+    pair_out, chip_out, src, tgt, adm = call(
         halo_kernel,
-        [payload, payload],
+        [payload, payload, lines, lines, weights],
         [pltpu.with_memory_space_constraint(x, pltpu.HBM) for x in (deviation, loading, tie_source, tie_target, tie_admittance)],
-        10.0,
+        0.1,
         [
             pltpu.VMEM((2, total, width), BF16),
             pltpu.VMEM((2, total, width), BF16),
-            pltpu.VMEM((blocks, edges), I32),
-            pltpu.VMEM((blocks, edges), I32),
-            pltpu.VMEM((blocks, edges), F32),
             pltpu.VMEM((TIE_ROWS, width), F32),
             pltpu.SemaphoreType.DMA((7,)),
         ],
         ins=[HBM] * 5,
     )
+    chip_out = call(pass_kernel, payload, (chip_out,), 10.0, aliases={0: 0})
     pairs = [(k, k ^ 1) for k in range(count)]
     groups = lax.axis_size("period")
     chips = []
@@ -319,7 +331,7 @@
     inner, ends, part = call(
         inner_kernel,
         [shape((blocks, total, width), BF16), shape((2, total, width), F32), shape((total, states_width), F32)],
-        (deviation, loading, jacobian, tie_source, tie_target, tie_admittance, condense),
+        (deviation, loading, jacobian, src, tgt, adm, condense),
         5.0,
         [pltpu.VMEM((blocks, total, width), BF16), pltpu.SemaphoreType.DMA],
         [HBM, VM, VM],
@@ -327,7 +339,7 @@
     outer, sums = call(
         ends_kernel,
         [shape((2, total, width), BF16), shape((total, states_width + 128), BF16)],
-        (deviation, loading, tie_source, tie_target, tie_admittance, condense, chip_in, pair_in, ends, part, retention[0]),
+        (deviation, loading, src, tgt, adm, condense, chip_in, pair_in, ends, part, retention[0]),
         1.0,
     )
     parts = lax.all_to_all(sums.reshape(count, rows, states_width + 128), "bus", 0, 0, tiled=True)

time: 28.5 us -> 28.4 us (level)
    pallas_call x5 -> x6, Pallas kernels: 4.53 us -> 4.29 us  [call(): pl.pallas_call(kernel, out_shape=shapes, in_specs=ins or [VM] * len(input...]
where the time goes in v6:
time: 28.4 us; the launch traced here: 28.1 us
  blocking collectives  19.9 us (70%)
  Pallas kernels  4.29 us (15%)
  starting transfers between devices  3.12 us (11%)
  between operations  0.75 us (3%)
    all_to_all x1, blocking collectives, shards(): everything = lax.all_to_all(sent, ('period', 'bus'), 0, 0, tiled=True)  11.2 us
    all_to_all x1, blocking collectives, shards(): lax.all_to_all(sums.reshape(count, rows, states_width + 128), 'bus', 0, 0...  8.7 us
    pallas_call x6, Pallas kernels, call(): pl.pallas_call(kernel, out_shape=shapes, in_specs=ins or [VM] * len(input...  4.29 us
    ppermute x1, starting transfers between devices, shards(): chip_in = lax.ppermute(chip_out, ('bus', 'period'), chips)  3.09 us
  transfers between devices with their start and end apart: 2, of which 0 were waited for; matrix products, arithmetic and copies ran while one was open for 0% of the time, Pallas kernels for 6%

profile of v6, /device:TPU:0, one launch (start us, length us, event | category | flops | bytes accessed | tf_op | source)
XLA Modules:
  0.0 28.1 jit_solution(9271130676081628283)
XLA Ops:
  0.6 0.9 %shard_map.104 = (bf16[80,128]{1,0:T(8,128)(2,1)S(1)}, bf16[80,128]{1,0:T(8,128)(2,1)S(1)}, s32[16,16]{1,0:T(8,128)S(1)}, s32[16,16]{1,0:T(8,128)S(1)}, f32[16,16]{1,0:T(8,128)S(1)}) custom-call(bf16[16,64,128]{2,1,0:T(8,128)(2,1)} %dev.3, bf16[16,64,128]{2,1,0:T(8,128)(2,1)} %load.3, s32[16,16]{1,0:T(8,128)} %src_hbm.1, s32[16,16]{1,0:T(8,128)} %tgt_hbm.1, ...), custom_call_target="tpu_custom_call" | custom-call | flops 100000000 | bytes 300000 | tf_op jit(solution)/shard_map/pallas_call | solution.py:283
  1.5 0.0 copy-start
  1.5 0.0 copy-start.1
  1.5 0.0 copy-start.3
  1.6 0.0 copy-start.4
  1.6 3.1 %collective-permute-start = (bf16[80,128]{1,0:T(8,128)(2,1)S(1)}, bf16[80,128]{1,0:T(8,128)(2,1)S(1)}, u32[]{:S(2)}, u32[]{:S(2)}) collective-permute-start(bf16[80,128]{1,0:T(8,128)(2,1)S(1)} %shard_map.105), channel_id=1, source_target_pairs={{0,1},{1,0},{2,3},{3,2},{4,8},{5,9},{6,10},{7,11},{8,4},{9,5},{10,... | collective-permute-start | bytes 61448 | tf_op jit(solution)/shard_map/ppermute | solution.py:329
  4.7 0.0 collective-permute-start.1
  4.7 0.0 copy-done
  4.7 0.0 copy-done.1
  4.7 0.0 copy-done.3
  4.7 0.0 copy-done.4
  4.7 0.0 copy-start.5
  4.7 0.0 copy-start.2
  4.7 1.7 %shard_map.106 = (bf16[16,64,128]{2,1,0:T(8,128)(2,1)}, f32[2,64,128]{2,1,0:T(8,128)S(1)}, f32[64,512]{1,0:T(8,128)S(1)}) custom-call(bf16[16,64,128]{2,1,0:T(8,128)(2,1)S(1)} %copy-done, bf16[16,64,128]{2,1,0:T(8,128)(2,1)S(1)} %copy-done.1, bf16[16,128,128]{2,1,0:T(8,128)(2,1)S(1)} %copy-done.4, s32[16,16]{1,0:T(8,128)S(1)} %get-tuple-element.18.src, ...), custom_call_target="tpu_custom_call" | custom-call | flops 5000000000 | bytes 15000000 | tf_op jit(solution)/shard_map/pallas_call | solution.py:283
  6.5 0.0 collective-permute-done.chip_in
  6.5 0.0 collective-permute-done.1.pair_in
  6.5 0.0 copy-done.5
  6.5 0.5 %shard_map.107 = (bf16[2,64,128]{2,1,0:T(8,128)(2,1)S(1)}, bf16[64,640]{1,0:T(8,128)(2,1)S(1)}) custom-call(bf16[16,64,128]{2,1,0:T(8,128)(2,1)S(1)} %copy-done, bf16[16,64,128]{2,1,0:T(8,128)(2,1)S(1)} %copy-done.1, s32[16,16]{1,0:T(8,128)S(1)} %get-tuple-element.18.src, s32[16,16]{1,0:T(8,128)S(1)} %get-tuple-element.19.tgt, ...), custom_call_target="tpu_custom_call" | custom-call | flops 1000000000 | bytes 3000000 | tf_op jit(solution)/shard_map/pallas_call | solution.py:283
  7.0 8.7 %all_to_all.10.parts = bf16[8,8,640]{2,1,0:T(8,128)(2,1)S(1)} all-to-all(bf16[8,8,640]{2,1,0:T(8,128)(2,1)S(1)} %bitcast.4), channel_id=1, replica_groups=mesh['bus'=8,'period'=4] {'bus'}, dimensions={0} | all-to-all | bytes 163840 | tf_op jit(solution)/shard_map/all_to_all | solution.py:345
  15.7 0.0 copy-done.2
  15.7 0.5 %shard_map.108 = (f32[8,512]{1,0:T(8,128)S(1)}, f32[8,512]{1,0:T(8,128)S(1)}, f32[8,4,128]{2,1,0:T(4,128)S(1)}, bf16[32,8,128]{2,1,0:T(8,128)(2,1)S(1)}) custom-call(bf16[8,8,640]{2,1,0:T(8,128)(2,1)S(1)} %all_to_all.10.parts, bf16[8,512,512]{2,1,0:T(8,128)(2,1)S(1)} %bitcast.5, f32[8,512]{1,0:T(8,128)S(1)} %bitcast.7), custom_call_target="tpu_custom_call" | custom-call | flops 2000000000 | bytes 6000000 | tf_op jit(solution)/shard_map/pallas_call | solution.py:283
  16.2 11.2 %all_to_all.11.spans = bf16[32,8,128]{2,1,0:T(8,128)(2,1)S(1)} all-to-all(bf16[32,8,128]{2,1,0:T(8,128)(2,1)S(1)} %get-tuple-element.26), channel_id=1, replica_groups=mesh['bus'=8,'period'=4] {'period','bus'}, dimensions={0} | all-to-all | bytes 131072 | tf_op jit(solution)/shard_map/all_to_all | solution.py:358
  27.4 0.7 %shard_map.109 = (f32[8,512]{1,0:T(8,128)}, bf16[16,64,128]{2,1,0:T(8,128)(2,1)}) custom-call(bf16[32,8,128]{2,1,0:T(8,128)(2,1)S(1)} %all_to_all.11.spans, f32[8,4,128]{2,1,0:T(4,128)S(1)} %get-tuple-element.27.rates, f32[8,512]{1,0:T(8,128)S(1)} %get-tuple-element.28.states, ...), custom_call_target="tpu_custom_call", output_to_operand_aliasing={{1}: (5, {})} | custom-call | flops 1000000000 | bytes 3000000 | tf_op jit(solution)/shard_map/pallas_call | solution.py:283
  (1 shorter events, 0.0 us)
Async XLA Ops:
  1.5 3.2 %copy-start = (bf16[16,64,128]{2,1,0:T(8,128)(2,1)S(1)}, bf16[16,64,128]{2,1,0:T(8,128)(2,1)}, u32[]{:S(2)}) copy-start(bf16[16,64,128]{2,1,0:T(8,128)(2,1)} %dev.3) | copy-start | bytes 786436
  1.5 3.2 %copy-start.1 = (bf16[16,64,128]{2,1,0:T(8,128)(2,1)S(1)}, bf16[16,64,128]{2,1,0:T(8,128)(2,1)}, u32[]{:S(2)}) copy-start(bf16[16,64,128]{2,1,0:T(8,128)(2,1)} %load.3) | copy-start | bytes 786436
  1.5 3.2 %copy-start.3 = (bf16[16,128,512]{2,1,0:T(8,128)(2,1)S(1)}, bf16[16,128,512]{2,1,0:T(8,128)(2,1)}, u32[]{:S(2)}) copy-start(bf16[16,128,512]{2,1,0:T(8,128)(2,1)} %cond.3) | copy-start | bytes 6291460
  1.6 3.2 %copy-start.4 = (bf16[16,128,128]{2,1,0:T(8,128)(2,1)S(1)}, bf16[16,128,128]{2,1,0:T(8,128)(2,1)}, u32[]{:S(2)}) copy-start(bf16[16,128,128]{2,1,0:T(8,128)(2,1)} %jac.1) | copy-start | bytes 1572868
  1.6 4.9 %collective-permute-start = (bf16[80,128]{1,0:T(8,128)(2,1)S(1)}, bf16[80,128]{1,0:T(8,128)(2,1)S(1)}, u32[]{:S(2)}, u32[]{:S(2)}) collective-permute-start(bf16[80,128]{1,0:T(8,128)(2,1)S(1)} %shard_map.105), channel_id=1, source_target_pairs={{0,1},{1,0},{2,3},{3,2},{4,8},{5,9},{6,10},{7,11},{8,4},{9,5},{10,... | collective-permute-start | bytes 61448 | tf_op jit(solution)/shard_map/ppermute | solution.py:329
  4.7 1.8 %collective-permute-start.1 = (bf16[80,128]{1,0:T(8,128)(2,1)S(1)}, bf16[80,128]{1,0:T(8,128)(2,1)S(1)}, u32[]{:S(2)}, u32[]{:S(2)}) collective-permute-start(bf16[80,128]{1,0:T(8,128)(2,1)S(1)} %get-tuple-element.22), channel_id=1, source_target_pairs={{0,4},{4,0},{8,12},{12,8},{16,20},{20,16},{24,28},{28,24},{1,5},{5... | collective-permute-start | bytes 61448 | tf_op jit(solution)/shard_map/ppermute | solution.py:330
  4.7 1.8 %copy-start.5 = (f32[1,8,512]{2,1,0:T(8,128)S(1)}, f32[1,8,512]{2,1,0:T(8,128)}, u32[]{:S(2)}) copy-start(f32[1,8,512]{2,1,0:T(8,128)} %param.17) | copy-start | bytes 49156
  4.7 11.0 %copy-start.2 = (bf16[1,8,512,512]{3,2,1,0:T(8,128)(2,1)S(1)}, bf16[1,8,512,512]{3,2,1,0:T(8,128)(2,1)}, u32[]{:S(2)}) copy-start(bf16[1,8,512,512]{3,2,1,0:T(8,128)(2,1)} %param.16) | copy-start | bytes 12582916

commit v7 on v5

--- a/solution.py
+++ b/solution.py
@@ -8,6 +8,7 @@
 F32, BF16, I32 = jnp.float32, jnp.bfloat16, jnp.int32
 VM = pl.BlockSpec(memory_space=pltpu.VMEM)
 TIE_ROWS = 16
+SUMMED_ROWS = 2
 PARAMS = pltpu.CompilerParams(vmem_limit_bytes=16 * 1024 * 1024)
 HBM = pl.BlockSpec(memory_space=pltpu.HBM)
 
@@ -202,9 +203,17 @@
 
     section_in = lax.fori_loop(0, count, add, jnp.zeros((rows, width), F32), unroll=8).astype(BF16)
     line = lax.broadcasted_iota(I32, (rows, width), 0)
+    columns = jnp.transpose(section_in.astype(F32))
     pushed = jnp.zeros((rows, width), F32)
     for r in range(rows):
-        pushed = jnp.where(line == r, dot(section_in, gain[r]), pushed)
+        if r < rows - SUMMED_ROWS:
+            row = dot(section_in, gain[r])
+        else:
+            row = jnp.zeros((16, width), F32)
+            for m in range(0, width, 16):
+                row = row + gain[r, m : m + 16, :].astype(F32) * columns[m : m + 16, r : r + 1]
+            row = jnp.sum(row, axis=0, keepdims=True)
+        pushed = jnp.where(line == r, row, pushed)
     rate, state = keep[...], pushed
     shift = 1
     while shift < rows:

time: 28.5 us -> 28.4 us (level)
  no operation moved by 1% of the time
where the time goes in v7:
time: 28.4 us; the launch traced here: 28.1 us
  blocking collectives  19.8 us (70%)
  Pallas kernels  4.41 us (16%)
  starting transfers between devices  3.12 us (11%)
  between operations  0.77 us (3%)
    all_to_all x1, blocking collectives, shards(): everything = lax.all_to_all(sent, ('period', 'bus'), 0, 0, tiled=True)  11.2 us
    all_to_all x1, blocking collectives, shards(): lax.all_to_all(sums.reshape(count, rows, states_width + 128), 'bus', 0, 0...  8.61 us
    pallas_call x5, Pallas kernels, call(): pl.pallas_call(kernel, out_shape=shapes, in_specs=ins or [VM] * len(input...  4.41 us
    ppermute x1, starting transfers between devices, shards(): chip_in = lax.ppermute(chip_out, ('bus', 'period'), chips)  3.09 us
  transfers between devices with their start and end apart: 2, of which 0 were waited for; matrix products, arithmetic and copies ran while one was open for 0% of the time, Pallas kernels for 6%

profile of v7, /device:TPU:0, one launch (start us, length us, event | category | flops | bytes accessed | tf_op | source)
XLA Modules:
  0.0 28.1 jit_solution(457025586024496976)
XLA Ops:
  0.6 0.0 copy-start.8
  0.6 0.0 copy-start.7
  0.7 0.0 copy-start.6
  0.7 0.0 copy-start.4
  0.7 0.0 copy-start.3
  0.7 0.0 copy-start.1
  0.7 0.0 copy-start.2
  0.7 1.0 %shard_map.104 = (bf16[80,128]{1,0:T(8,128)(2,1)S(1)}, bf16[80,128]{1,0:T(8,128)(2,1)S(1)}) custom-call(bf16[16,64,128]{2,1,0:T(8,128)(2,1)} %dev.3, bf16[16,64,128]{2,1,0:T(8,128)(2,1)} %load.3, s32[16,16]{1,0:T(8,128)} %src.3, s32[16,16]{1,0:T(8,128)} %tgt.3, f32[16,16]{1,0:T(8,128)} %adm.3), custom_call_target="tpu_custom_call" | custom-call | flops 10000000000 | bytes 30000000 | tf_op jit(solution)/shard_map/pallas_call | solution.py:279
  1.7 3.1 %collective-permute-start = (bf16[80,128]{1,0:T(8,128)(2,1)S(1)}, bf16[80,128]{1,0:T(8,128)(2,1)S(1)}, u32[]{:S(2)}, u32[]{:S(2)}) collective-permute-start(bf16[80,128]{1,0:T(8,128)(2,1)S(1)} %get-tuple-element.15), channel_id=1, source_target_pairs={{0,1},{1,0},{2,3},{3,2},{4,8},{5,9},{6,10},{7,11},{8,4},{9,5},{10,... | collective-permute-start | bytes 61448 | tf_op jit(solution)/shard_map/ppermute | solution.py:326
  4.8 0.0 copy-start.5
  4.8 0.0 copy-start
  4.8 0.0 collective-permute-start.1
  4.8 0.0 copy-done.8
  4.8 0.0 copy-done.7
  4.8 0.0 copy-done.6
  4.8 0.0 copy-done.4
  4.8 0.0 copy-done.3
  4.9 0.0 copy-done.1
  4.9 0.0 copy-done.2
  4.9 1.7 %shard_map.105 = (bf16[16,64,128]{2,1,0:T(8,128)(2,1)}, f32[2,64,128]{2,1,0:T(8,128)S(1)}, f32[64,512]{1,0:T(8,128)S(1)}) custom-call(bf16[16,64,128]{2,1,0:T(8,128)(2,1)S(1)} %copy-done.3, bf16[16,64,128]{2,1,0:T(8,128)(2,1)S(1)} %copy-done.4, bf16[16,128,128]{2,1,0:T(8,128)(2,1)S(1)} %copy-done.2, s32[16,16]{1,0:T(8,128)S(1)} %copy-done.6, ...), custom_call_target="tpu_custom_call" | custom-call | flops 5000000000 | bytes 15000000 | tf_op jit(solution)/shard_map/pallas_call | solution.py:279
  6.6 0.0 collective-permute-done.chip_in
  6.6 0.0 collective-permute-done.1.pair_in
  6.6 0.0 copy-done.5
  6.6 0.5 %shard_map.106 = (bf16[2,64,128]{2,1,0:T(8,128)(2,1)S(1)}, bf16[64,640]{1,0:T(8,128)(2,1)S(1)}) custom-call(bf16[16,64,128]{2,1,0:T(8,128)(2,1)S(1)} %copy-done.3, bf16[16,64,128]{2,1,0:T(8,128)(2,1)S(1)} %copy-done.4, s32[16,16]{1,0:T(8,128)S(1)} %copy-done.6, s32[16,16]{1,0:T(8,128)S(1)} %copy-done.7, f32[16,16]{1,0:T(8,128)S(1)} %copy-done.8, ...), custom_call_target="tpu_custom_call" | custom-call | flops 1000000000 | bytes 3000000 | tf_op jit(solution)/shard_map/pallas_call | solution.py:279
  7.1 8.6 %all_to_all.10.parts = bf16[8,8,640]{2,1,0:T(8,128)(2,1)S(1)} all-to-all(bf16[8,8,640]{2,1,0:T(8,128)(2,1)S(1)} %bitcast.4), channel_id=1, replica_groups=mesh['bus'=8,'period'=4] {'bus'}, dimensions={0} | all-to-all | bytes 163840 | tf_op jit(solution)/shard_map/all_to_all | solution.py:342
  15.7 0.0 copy-done
  15.7 0.5 %shard_map.107 = (f32[8,512]{1,0:T(8,128)S(1)}, f32[8,512]{1,0:T(8,128)S(1)}, f32[8,4,128]{2,1,0:T(4,128)S(1)}, bf16[32,8,128]{2,1,0:T(8,128)(2,1)S(1)}) custom-call(bf16[8,8,640]{2,1,0:T(8,128)(2,1)S(1)} %all_to_all.10.parts, bf16[8,512,512]{2,1,0:T(8,128)(2,1)S(1)} %bitcast.5, f32[8,512]{1,0:T(8,128)S(1)} %bitcast.7), custom_call_target="tpu_custom_call" | custom-call | flops 2000000000 | bytes 6000000 | tf_op jit(solution)/shard_map/pallas_call | solution.py:279
  16.3 11.2 %all_to_all.11.spans = bf16[32,8,128]{2,1,0:T(8,128)(2,1)S(1)} all-to-all(bf16[32,8,128]{2,1,0:T(8,128)(2,1)S(1)} %get-tuple-element.20), channel_id=1, replica_groups=mesh['bus'=8,'period'=4] {'period','bus'}, dimensions={0} | all-to-all | bytes 131072 | tf_op jit(solution)/shard_map/all_to_all | solution.py:355
  27.5 0.7 %shard_map.108 = (f32[8,512]{1,0:T(8,128)}, bf16[16,64,128]{2,1,0:T(8,128)(2,1)}) custom-call(bf16[32,8,128]{2,1,0:T(8,128)(2,1)S(1)} %all_to_all.11.spans, f32[8,4,128]{2,1,0:T(4,128)S(1)} %get-tuple-element.21.rates, f32[8,512]{1,0:T(8,128)S(1)} %get-tuple-element.22.states, ...), custom_call_target="tpu_custom_call", output_to_operand_aliasing={{1}: (5, {})} | custom-call | flops 1000000000 | bytes 3000000 | tf_op jit(solution)/shard_map/pallas_call | solution.py:279
Async XLA Ops:
  0.6 4.2 %copy-start.8 = (f32[16,16]{1,0:T(8,128)S(1)}, f32[16,16]{1,0:T(8,128)}, u32[]{:S(2)}) copy-start(f32[16,16]{1,0:T(8,128)} %adm.3) | copy-start | bytes 3076
  0.6 4.2 %copy-start.7 = (s32[16,16]{1,0:T(8,128)S(1)}, s32[16,16]{1,0:T(8,128)}, u32[]{:S(2)}) copy-start(s32[16,16]{1,0:T(8,128)} %tgt.3) | copy-start | bytes 3076
  0.7 4.2 %copy-start.6 = (s32[16,16]{1,0:T(8,128)S(1)}, s32[16,16]{1,0:T(8,128)}, u32[]{:S(2)}) copy-start(s32[16,16]{1,0:T(8,128)} %src.3) | copy-start | bytes 3076
  0.7 4.2 %copy-start.4 = (bf16[16,64,128]{2,1,0:T(8,128)(2,1)S(1)}, bf16[16,64,128]{2,1,0:T(8,128)(2,1)}, u32[]{:S(2)}) copy-start(bf16[16,64,128]{2,1,0:T(8,128)(2,1)} %load.3) | copy-start | bytes 786436
  0.7 4.2 %copy-start.3 = (bf16[16,64,128]{2,1,0:T(8,128)(2,1)S(1)}, bf16[16,64,128]{2,1,0:T(8,128)(2,1)}, u32[]{:S(2)}) copy-start(bf16[16,64,128]{2,1,0:T(8,128)(2,1)} %dev.3) | copy-start | bytes 786436
  0.7 4.2 %copy-start.1 = (bf16[16,128,512]{2,1,0:T(8,128)(2,1)S(1)}, bf16[16,128,512]{2,1,0:T(8,128)(2,1)}, u32[]{:S(2)}) copy-start(bf16[16,128,512]{2,1,0:T(8,128)(2,1)} %cond.3) | copy-start | bytes 6291460
  0.7 4.2 %copy-start.2 = (bf16[16,128,128]{2,1,0:T(8,128)(2,1)S(1)}, bf16[16,128,128]{2,1,0:T(8,128)(2,1)}, u32[]{:S(2)}) copy-start(bf16[16,128,128]{2,1,0:T(8,128)(2,1)} %jac.1) | copy-start | bytes 1572868
  1.7 4.9 %collective-permute-start = (bf16[80,128]{1,0:T(8,128)(2,1)S(1)}, bf16[80,128]{1,0:T(8,128)(2,1)S(1)}, u32[]{:S(2)}, u32[]{:S(2)}) collective-permute-start(bf16[80,128]{1,0:T(8,128)(2,1)S(1)} %get-tuple-element.15), channel_id=1, source_target_pairs={{0,1},{1,0},{2,3},{3,2},{4,8},{5,9},{6,10},{7,11},{8,4},{9,5},{10,... | collective-permute-start | bytes 61448 | tf_op jit(solution)/shard_map/ppermute | solution.py:326
  4.8 1.8 %copy-start.5 = (f32[1,8,512]{2,1,0:T(8,128)S(1)}, f32[1,8,512]{2,1,0:T(8,128)}, u32[]{:S(2)}) copy-start(f32[1,8,512]{2,1,0:T(8,128)} %param.17) | copy-start | bytes 49156
  4.8 10.9 %copy-start = (bf16[1,8,512,512]{3,2,1,0:T(8,128)(2,1)S(1)}, bf16[1,8,512,512]{3,2,1,0:T(8,128)(2,1)}, u32[]{:S(2)}) copy-start(bf16[1,8,512,512]{3,2,1,0:T(8,128)(2,1)} %param.16) | copy-start | bytes 12582916
  4.8 1.8 %collective-permute-start.1 = (bf16[80,128]{1,0:T(8,128)(2,1)S(1)}, bf16[80,128]{1,0:T(8,128)(2,1)S(1)}, u32[]{:S(2)}, u32[]{:S(2)}) collective-permute-start(bf16[80,128]{1,0:T(8,128)(2,1)S(1)} %get-tuple-element.16), channel_id=1, source_target_pairs={{0,4},{4,0},{8,12},{12,8},{16,20},{20,16},{24,28},{28,24},{1,5},{5... | collective-permute-start | bytes 61448 | tf_op jit(solution)/shard_map/ppermute | solution.py:327

commit v8 on v6

--- a/solution.py
+++ b/solution.py
@@ -99,7 +99,7 @@
     same[0:8, :] = given[0:8, :]
 
 
-def inner_kernel(dev, load, jac, src, tgt, adm, cond, mis_hbm, ends, part, mis, sem):
+def inner_kernel(dev, load, jac, src, tgt, adm, cond, mis_hbm, mis, ends, part, sem):
     blocks, total, width = dev.shape
     edges = src.shape[1]
     src4 = jnp.concatenate([src[...]] * 4, axis=1)
@@ -132,9 +132,10 @@
                 rounded = whole.astype(BF16)
                 mis[b, here, :] = rounded
                 row.append((b, rounded))
-        middle = pl.ds(1, blocks - 2)
-        copy = pltpu.make_async_copy(mis.at[middle, here, :], mis_hbm.at[middle, here, :], sem)
-        copy.start()
+            if b == blocks // 2 - 1:
+                early = pl.ds(1, b)
+                copy = pltpu.make_async_copy(mis.at[early, here, :], mis_hbm.at[early, here, :], sem)
+                copy.start()
         sums = 0.0
         for k in range(0, len(row), 2):
             pair = row[k : k + 2]
@@ -248,9 +249,11 @@
             sent[q * count + k] = value
 
 
-def enter_kernel(spans, rates, states, running, outer, mis_in, out_hbm, mis, out, sems):
+def enter_kernel(spans, rates, states, running, outer, inner, mis_in, out_hbm, mis, out, sems):
     blocks = mis.shape[0]
-    copies = [pltpu.make_async_copy(outer.at[k], mis.at[k * (blocks - 1)], sems.at[k]) for k in range(2)]
+    late = pl.ds(blocks // 2, blocks - 1 - blocks // 2)
+    copies = [pltpu.make_async_copy(inner.at[late], mis.at[late], sems.at[0])]
+    copies += [pltpu.make_async_copy(outer.at[k], mis.at[k * (blocks - 1)], sems.at[k + 1]) for k in range(2)]
     for copy in copies:
         copy.start()
     count, tiles, _ = rates.shape
@@ -272,8 +275,8 @@
 
     entering = lax.fori_loop(0, count, step, entering, unroll=8)
     out[...] = states[...] + running[...] * unfolded(entering)
-    copies.append(pltpu.make_async_copy(out, out_hbm, sems.at[2]))
-    copies[2].start()
+    copies.append(pltpu.make_async_copy(out, out_hbm, sems.at[3]))
+    copies[3].start()
     for copy in copies:
         copy.wait()
 
@@ -328,13 +331,13 @@
                 chips.append((k * groups + g, k * groups + g ^ 1))
     chip_in = lax.ppermute(chip_out, ("bus", "period"), chips)
     pair_in = lax.ppermute(pair_out, "bus", pairs)
-    inner, ends, part = call(
+    early, inner, ends, part = call(
         inner_kernel,
-        [shape((blocks, total, width), BF16), shape((2, total, width), F32), shape((total, states_width), F32)],
+        [shape((blocks, total, width), BF16), shape((blocks, total, width), BF16), shape((2, total, width), F32), shape((total, states_width), F32)],
         (deviation, loading, jacobian, src, tgt, adm, condense),
         5.0,
-        [pltpu.VMEM((blocks, total, width), BF16), pltpu.SemaphoreType.DMA],
-        [HBM, VM, VM],
+        [pltpu.SemaphoreType.DMA],
+        [HBM, VM, VM, VM],
     )
     outer, sums = call(
         ends_kernel,
@@ -359,12 +362,12 @@
     out, mismatch = call(
         enter_kernel,
         [shape((rows, states_width), F32), shape((blocks, total, width), BF16)],
-        (everything, rates, states, running, outer, inner),
+        (everything, rates, states, running, outer, inner, early),
         1.0,
-        [pltpu.VMEM((rows, states_width), F32), pltpu.SemaphoreType.DMA((3,))],
+        [pltpu.VMEM((rows, states_width), F32), pltpu.SemaphoreType.DMA((4,))],
         [HBM, HBM],
-        [VM] * 5 + [HBM],
-        {5: 1},
+        [VM] * 6 + [HBM],
+        {6: 1},
     )
     return (mismatch, out[None])
 

time: 28.4 us -> 28.4 us (level)
  Pallas kernels: 4.29 us -> 4 us
    pallas_call x6, Pallas kernels: 4.29 us -> 4 us  [call(): pl.pallas_call(kernel, out_shape=shapes, in_specs=ins or [VM] * len(input...]
  transfers between devices with their start and end apart: 2 -> 2, of which waited for: 0 -> 1; matrix products, arithmetic and copies ran while one was open for 0% -> 0% of each run, Pallas kernels for 6% -> 5%
where the time goes in v8:
time: 28.4 us; the launch traced here: 28 us
  blocking collectives  19.9 us (70%)
  Pallas kernels  4 us (14%)
  starting transfers between devices  3.12 us (11%)
  between operations  0.73 us (3%)
  waiting for transfers between devices  0.29 us (1%)
    all_to_all x1, blocking collectives, shards(): everything = lax.all_to_all(sent, ('period', 'bus'), 0, 0, tiled=True)  11.2 us
    all_to_all x1, blocking collectives, shards(): lax.all_to_all(sums.reshape(count, rows, states_width + 128), 'bus', 0, 0...  8.67 us
    pallas_call x6, Pallas kernels, call(): pl.pallas_call(kernel, out_shape=shapes, in_specs=ins or [VM] * len(input...  4 us
    ppermute x1, starting transfers between devices, shards(): chip_in = lax.ppermute(chip_out, ('bus', 'period'), chips)  3.09 us
  transfers between devices with their start and end apart: 2, of which 1 were waited for; matrix products, arithmetic and copies ran while one was open for 0% of the time, Pallas kernels for 5%

profile of v8, /device:TPU:0, one launch (start us, length us, event | category | flops | bytes accessed | tf_op | source)
XLA Modules:
  0.0 28.0 jit_solution(8927164236737722295)
XLA Ops:
  0.6 0.9 %shard_map.104 = (bf16[80,128]{1,0:T(8,128)(2,1)S(1)}, bf16[80,128]{1,0:T(8,128)(2,1)S(1)}, s32[16,16]{1,0:T(8,128)S(1)}, s32[16,16]{1,0:T(8,128)S(1)}, f32[16,16]{1,0:T(8,128)S(1)}) custom-call(bf16[16,64,128]{2,1,0:T(8,128)(2,1)} %dev.3, bf16[16,64,128]{2,1,0:T(8,128)(2,1)} %load.3, s32[16,16]{1,0:T(8,128)} %src_hbm.1, s32[16,16]{1,0:T(8,128)} %tgt_hbm.1, ...), custom_call_target="tpu_custom_call" | custom-call | flops 100000000 | bytes 300000 | tf_op jit(solution)/shard_map/pallas_call | solution.py:286
  1.5 0.0 copy-start
  1.5 0.0 copy-start.1
  1.5 0.0 copy-start.3
  1.6 0.0 copy-start.4
  1.6 3.1 %collective-permute-start = (bf16[80,128]{1,0:T(8,128)(2,1)S(1)}, bf16[80,128]{1,0:T(8,128)(2,1)S(1)}, u32[]{:S(2)}, u32[]{:S(2)}) collective-permute-start(bf16[80,128]{1,0:T(8,128)(2,1)S(1)} %shard_map.105), channel_id=1, source_target_pairs={{0,1},{1,0},{2,3},{3,2},{4,8},{5,9},{6,10},{7,11},{8,4},{9,5},{10,... | collective-permute-start | bytes 61448 | tf_op jit(solution)/shard_map/ppermute | solution.py:332
  4.7 0.0 collective-permute-start.1
  4.7 0.0 copy-done
  4.7 0.0 copy-done.1
  4.7 0.0 copy-done.3
  4.7 0.0 copy-done.4
  4.7 0.0 copy-start.5
  4.7 0.0 copy-start.2
  4.7 1.4 %shard_map.106 = (bf16[16,64,128]{2,1,0:T(8,128)(2,1)}, bf16[16,64,128]{2,1,0:T(8,128)(2,1)S(1)}, f32[2,64,128]{2,1,0:T(8,128)S(1)}, f32[64,512]{1,0:T(8,128)S(1)}) custom-call(bf16[16,64,128]{2,1,0:T(8,128)(2,1)S(1)} %copy-done, bf16[16,64,128]{2,1,0:T(8,128)(2,1)S(1)} %copy-done.1, bf16[16,128,128]{2,1,0:T(8,128)(2,1)S(1)} %copy-done.4, ...), custom_call_target="tpu_custom_call" | custom-call | flops 5000000000 | bytes 15000000 | tf_op jit(solution)/shard_map/pallas_call | solution.py:286
  6.1 0.3 %collective-permute-done.chip_in = bf16[80,128]{1,0:T(8,128)(2,1)S(1)} collective-permute-done((bf16[80,128]{1,0:T(8,128)(2,1)S(1)}, bf16[80,128]{1,0:T(8,128)(2,1)S(1)}, u32[]{:S(2)}, u32[]{:S(2)}) %collective-permute-start) | collective-permute-done | bytes 20512 | tf_op jit(solution)/shard_map/ppermute | solution.py:332
  6.4 0.0 collective-permute-done.1.pair_in
  6.4 0.0 copy-done.5
  6.4 0.5 %shard_map.107 = (bf16[2,64,128]{2,1,0:T(8,128)(2,1)S(1)}, bf16[64,640]{1,0:T(8,128)(2,1)S(1)}) custom-call(bf16[16,64,128]{2,1,0:T(8,128)(2,1)S(1)} %copy-done, bf16[16,64,128]{2,1,0:T(8,128)(2,1)S(1)} %copy-done.1, s32[16,16]{1,0:T(8,128)S(1)} %get-tuple-element.19.src, s32[16,16]{1,0:T(8,128)S(1)} %get-tuple-element.20.tgt, ...), custom_call_target="tpu_custom_call" | custom-call | flops 1000000000 | bytes 3000000 | tf_op jit(solution)/shard_map/pallas_call | solution.py:286
  6.9 8.7 %all_to_all.10.parts = bf16[8,8,640]{2,1,0:T(8,128)(2,1)S(1)} all-to-all(bf16[8,8,640]{2,1,0:T(8,128)(2,1)S(1)} %bitcast.4), channel_id=1, replica_groups=mesh['bus'=8,'period'=4] {'bus'}, dimensions={0} | all-to-all | bytes 163840 | tf_op jit(solution)/shard_map/all_to_all | solution.py:348
  15.6 0.0 copy-done.2
  15.6 0.5 %shard_map.108 = (f32[8,512]{1,0:T(8,128)S(1)}, f32[8,512]{1,0:T(8,128)S(1)}, f32[8,4,128]{2,1,0:T(4,128)S(1)}, bf16[32,8,128]{2,1,0:T(8,128)(2,1)S(1)}) custom-call(bf16[8,8,640]{2,1,0:T(8,128)(2,1)S(1)} %all_to_all.10.parts, bf16[8,512,512]{2,1,0:T(8,128)(2,1)S(1)} %bitcast.5, f32[8,512]{1,0:T(8,128)S(1)} %bitcast.7), custom_call_target="tpu_custom_call" | custom-call | flops 2000000000 | bytes 6000000 | tf_op jit(solution)/shard_map/pallas_call | solution.py:286
  16.1 11.2 %all_to_all.11.spans = bf16[32,8,128]{2,1,0:T(8,128)(2,1)S(1)} all-to-all(bf16[32,8,128]{2,1,0:T(8,128)(2,1)S(1)} %get-tuple-element.27), channel_id=1, replica_groups=mesh['bus'=8,'period'=4] {'period','bus'}, dimensions={0} | all-to-all | bytes 131072 | tf_op jit(solution)/shard_map/all_to_all | solution.py:361
  27.3 0.7 %shard_map.109 = (f32[8,512]{1,0:T(8,128)}, bf16[16,64,128]{2,1,0:T(8,128)(2,1)}) custom-call(bf16[32,8,128]{2,1,0:T(8,128)(2,1)S(1)} %all_to_all.11.spans, f32[8,4,128]{2,1,0:T(4,128)S(1)} %get-tuple-element.28.rates, f32[8,512]{1,0:T(8,128)S(1)} %get-tuple-element.29.states, ...), custom_call_target="tpu_custom_call", output_to_operand_aliasing={{1}: (6, {})} | custom-call | flops 1000000000 | bytes 3000000 | tf_op jit(solution)/shard_map/pallas_call | solution.py:286
  (1 shorter events, 0.0 us)
Async XLA Ops:
  1.5 3.2 %copy-start = (bf16[16,64,128]{2,1,0:T(8,128)(2,1)S(1)}, bf16[16,64,128]{2,1,0:T(8,128)(2,1)}, u32[]{:S(2)}) copy-start(bf16[16,64,128]{2,1,0:T(8,128)(2,1)} %dev.3) | copy-start | bytes 786436
  1.5 3.2 %copy-start.1 = (bf16[16,64,128]{2,1,0:T(8,128)(2,1)S(1)}, bf16[16,64,128]{2,1,0:T(8,128)(2,1)}, u32[]{:S(2)}) copy-start(bf16[16,64,128]{2,1,0:T(8,128)(2,1)} %load.3) | copy-start | bytes 786436
  1.5 3.2 %copy-start.3 = (bf16[16,128,512]{2,1,0:T(8,128)(2,1)S(1)}, bf16[16,128,512]{2,1,0:T(8,128)(2,1)}, u32[]{:S(2)}) copy-start(bf16[16,128,512]{2,1,0:T(8,128)(2,1)} %cond.3) | copy-start | bytes 6291460
  1.6 3.2 %copy-start.4 = (bf16[16,128,128]{2,1,0:T(8,128)(2,1)S(1)}, bf16[16,128,128]{2,1,0:T(8,128)(2,1)}, u32[]{:S(2)}) copy-start(bf16[16,128,128]{2,1,0:T(8,128)(2,1)} %jac.1) | copy-start | bytes 1572868
  1.6 4.9 %collective-permute-start = (bf16[80,128]{1,0:T(8,128)(2,1)S(1)}, bf16[80,128]{1,0:T(8,128)(2,1)S(1)}, u32[]{:S(2)}, u32[]{:S(2)}) collective-permute-start(bf16[80,128]{1,0:T(8,128)(2,1)S(1)} %shard_map.105), channel_id=1, source_target_pairs={{0,1},{1,0},{2,3},{3,2},{4,8},{5,9},{6,10},{7,11},{8,4},{9,5},{10,... | collective-permute-start | bytes 61448 | tf_op jit(solution)/shard_map/ppermute | solution.py:332
  4.7 1.8 %collective-permute-start.1 = (bf16[80,128]{1,0:T(8,128)(2,1)S(1)}, bf16[80,128]{1,0:T(8,128)(2,1)S(1)}, u32[]{:S(2)}, u32[]{:S(2)}) collective-permute-start(bf16[80,128]{1,0:T(8,128)(2,1)S(1)} %get-tuple-element.23), channel_id=1, source_target_pairs={{0,4},{4,0},{8,12},{12,8},{16,20},{20,16},{24,28},{28,24},{1,5},{5... | collective-permute-start | bytes 61448 | tf_op jit(solution)/shard_map/ppermute | solution.py:333
  4.7 1.7 %copy-start.5 = (f32[1,8,512]{2,1,0:T(8,128)S(1)}, f32[1,8,512]{2,1,0:T(8,128)}, u32[]{:S(2)}) copy-start(f32[1,8,512]{2,1,0:T(8,128)} %param.17) | copy-start | bytes 49156
  4.7 10.9 %copy-start.2 = (bf16[1,8,512,512]{3,2,1,0:T(8,128)(2,1)S(1)}, bf16[1,8,512,512]{3,2,1,0:T(8,128)(2,1)}, u32[]{:S(2)}) copy-start(bf16[1,8,512,512]{3,2,1,0:T(8,128)(2,1)} %param.16) | copy-start | bytes 12582916
